TPU v7x, 32 devices: a whole 2x2x4 slice. The times are simulated.
32 devices in a mesh: section: 2 (over core), seq: 4 (over z), chan: 4 (over y, x).
Axes of the slice: x: 2, y: 2, z: 4, core: 2. Of those that a mesh axis runs over, the one named last changes fastest.
Arguments:
- inputs: bfloat16 [2, 256, 4096], P(None, 'seq', 'chan'), may hold values from -8 to 8
- out_grad: bfloat16 [2, 256, 4096], P(None, 'seq', 'chan'), may hold values from -0.625 to 0.625
- short_filters: float32 [2, 3, 7, 4096], P('section', None, None, 'chan'), may hold values from -2 to 2
- long_filters: float32 [2, 128, 4096], P('section', None, 'chan'), may hold values from -0.5 to 0.5
- skip_gain: float32 [2, 4096], P('section', 'chan'), may hold values from -1 to 1
- norm_gain: float32 [2, 4096], P('section', 'chan'), may hold values from 0.5 to 1.5
Outputs:
- param_grads: float32 [2, 151, 4096], P('section', None, 'chan')
All inputs are finite; a program needn't handle non-finite values.
Results may differ from a plain program's by a relative error of at most 0.012.
The roundings to bfloat16 on the way count: a program that leaves them out, or rounds other values in their place, can miss the bound.
Values may be sent and summed in bfloat16 or wider, within the bound.
A program may use at most 64 MiB of HBM per device.

v0:
```python
import jax
import jax.numpy as jnp
from jax import lax
from jax.sharding import PartitionSpec as P

D = 4096


EPSILON = 1e-06


def shifted(block, axis, distance):
    devices = range(lax.axis_size(axis))
    route = [(i - distance, i) for i in devices if i - distance in devices]
    return lax.ppermute(block, axis, route)


def as_sent(array):
    return jax.tree.map(lambda a: a.astype(jnp.bfloat16) if a.dtype == jnp.float32 else a, array)


def correlate(signal, filters):
    result = lax.conv_general_dilated(
        signal[None],
        filters[:, None, :],
        (1,),
        "VALID",
        dimension_numbers=("NWC", "WIO", "NWC"),
        feature_group_count=signal.shape[1],
        precision=lax.Precision.HIGHEST,
    )
    return result[0]


def rows_before(source_rows, wanted, sender):
    row_count = source_rows.shape[0]
    hop_count = (wanted + row_count - 1) // row_count
    pieces = []
    for distance in range(hop_count, 0, -1):
        taking = min(row_count, wanted - (distance - 1) * row_count)
        pieces.append(sender(source_rows[row_count - taking :], distance))
    return jnp.concatenate(pieces, axis=0)


def rows_after(source_rows, wanted, sender):
    row_count = source_rows.shape[0]
    hop_count = (wanted + row_count - 1) // row_count
    pieces = []
    for distance in range(1, hop_count + 1):
        taking = min(row_count, wanted - (distance - 1) * row_count)
        pieces.append(sender(source_rows[:taking], distance))
    return jnp.concatenate(pieces, axis=0)


def forward_layer(x_rows, short_taps, long_taps, skip_row, gain_row):
    short_len = short_taps.shape[1]
    long_len = long_taps.shape[0]
    x_float = x_rows.astype(jnp.float32)
    squares = lax.psum(jnp.sum(x_float * x_float, axis=1), "chan")
    scale = lax.rsqrt(squares / D + EPSILON)
    normed = (x_float * scale[:, None] * gain_row).astype(jnp.bfloat16)
    h_before = rows_before(
        normed, short_len - 1, lambda shard_rows, distance: shifted(shard_rows, "seq", distance)
    )
    h_extended = jnp.concatenate([h_before, normed], axis=0)
    h_float = h_extended.astype(jnp.float32)
    query = correlate(h_float, short_taps[0][::-1])
    key_rows = correlate(h_float, short_taps[1][::-1])
    value_rows = correlate(h_float, short_taps[2][::-1])
    mixed = (key_rows * value_rows).astype(jnp.bfloat16)
    z_before = rows_before(
        mixed,
        long_len - 1,
        lambda shard_rows, distance: jax.tree.map(
            lambda part, own: part.astype(own.dtype),
            shifted(as_sent(shard_rows), "seq", distance),
            shard_rows,
        ),
    )
    z_extended = jnp.concatenate([z_before, mixed], axis=0)
    mixed_float = z_extended.astype(jnp.float32)
    filtered = correlate(mixed_float, long_taps[::-1]) + skip_row * mixed_float[long_len - 1 :]
    x_next = (x_float + query * filtered).astype(jnp.bfloat16)
    return (x_next, (x_rows, h_extended, z_extended, scale))


def backward_layer(e_rows, stored, short_taps, long_taps, skip_row, gain_row):
    short_len = short_taps.shape[1]
    long_len = long_taps.shape[0]
    x_bf, h_bf, z_bf, scale = stored
    row_count = x_bf.shape[0]
    x_float = x_bf.astype(jnp.float32)
    h_float = h_bf.astype(jnp.float32)
    z_float = z_bf.astype(jnp.float32)
    query = correlate(h_float, short_taps[0][::-1])
    key_rows = correlate(h_float, short_taps[1][::-1])
    value_rows = correlate(h_float, short_taps[2][::-1])
    mixed_float = z_float[long_len - 1 :]
    filtered = correlate(z_float, long_taps[::-1]) + skip_row * mixed_float
    e_float = e_rows.astype(jnp.float32)
    d_query = (e_float * filtered).astype(jnp.bfloat16)
    d_filtered = (e_float * query).astype(jnp.bfloat16)
    filtered_after = rows_after(
        d_filtered, long_len - 1, lambda shard_rows, distance: shifted(shard_rows, "seq", -distance)
    )
    filtered_float = jnp.concatenate([d_filtered, filtered_after], axis=0).astype(jnp.float32)
    d_mixed = correlate(filtered_float, long_taps) + skip_row * filtered_float[:row_count]
    d_key = (d_mixed * value_rows).astype(jnp.bfloat16)
    d_value = (d_mixed * key_rows).astype(jnp.bfloat16)
    streams = jnp.stack([d_query, d_key, d_value], axis=1)
    streams_after = rows_after(
        streams, short_len - 1, lambda shard_rows, distance: shifted(shard_rows, "seq", -distance)
    )
    streams_float = jnp.concatenate([streams, streams_after], axis=0).astype(jnp.float32)
    d_normed = correlate(streams_float[:, 0], short_taps[0])
    d_normed = d_normed + correlate(streams_float[:, 1], short_taps[1])
    d_normed = d_normed + correlate(streams_float[:, 2], short_taps[2])
    fresh = jnp.concatenate(
        [
            correlate(h_float, streams_float[:row_count, 0])[::-1],
            correlate(h_float, streams_float[:row_count, 1])[::-1],
            correlate(h_float, streams_float[:row_count, 2])[::-1],
            correlate(z_float, filtered_float[:row_count])[::-1],
            jnp.sum(filtered_float[:row_count] * mixed_float, axis=0)[None],
            jnp.sum(d_normed * x_float * scale[:, None], axis=0)[None],
        ],
        axis=0,
    )
    norm_term = lax.psum(jnp.sum(gain_row * d_normed * x_float, axis=1), "chan") / D
    e_prev = (
        e_float
        + scale[:, None] * gain_row * d_normed
        - x_float * (scale * scale * scale)[:, None] * norm_term[:, None]
    ).astype(jnp.bfloat16)
    return (e_prev, fresh)


def on_device(inputs, out_grad, short_filters, long_filters, skip_gain, norm_gain):
    sections = lax.axis_size("section")
    section_index = lax.axis_index("section")
    micro_count, row_count, channels = inputs.shape
    short_len = short_filters.shape[2]
    long_len = long_filters.shape[1]
    param_rows = 3 * short_len + long_len + 2
    gathered = (
        lax.all_gather(short_filters, "section", axis=0, tiled=True),
        lax.all_gather(long_filters, "section", axis=0, tiled=True),
        lax.all_gather(skip_gain, "section", axis=0, tiled=True),
        lax.all_gather(norm_gain, "section", axis=0, tiled=True),
    )
    layer_count = gathered[0].shape[0]
    per_device = micro_count // sections
    own_inputs = lax.dynamic_slice_in_dim(inputs, section_index * per_device, per_device, 0)
    own_grads = lax.dynamic_slice_in_dim(out_grad, section_index * per_device, per_device, 0)

    def one_micro(grad_total, micro_rows):
        first_rows, top_grad = micro_rows

        def forward_pass(x_rows, params):
            return forward_layer(x_rows, params[0], params[1], params[2], params[3])

        x_final, stored_all = lax.scan(forward_pass, first_rows, gathered)

        def backward_pass(e_rows, layer_items):
            params, stored = layer_items
            return backward_layer(e_rows, stored, params[0], params[1], params[2], params[3])

        e_first, fresh_all = lax.scan(backward_pass, top_grad, (gathered, stored_all), reverse=True)
        return (grad_total + fresh_all, None)

    grads_start = jnp.zeros((layer_count, param_rows, channels), jnp.float32)
    grads_done, unused_micro = lax.scan(one_micro, grads_start, (own_inputs, own_grads))
    local_grads = lax.psum_scatter(grads_done, "section", scatter_dimension=0, tiled=True)
    return lax.psum(local_grads, "seq")


def solution(mesh):
    placed = (
        P(None, "seq", "chan"),
        P(None, "seq", "chan"),
        P("section", None, None, "chan"),
        P("section", None, "chan"),
        P("section", "chan"),
        P("section", "chan"),
    )
    return jax.shard_map(
        on_device, mesh=mesh, in_specs=placed, out_specs=P("section", None, "chan"), check_vma=False
    )
```

profile of v0, /device:TPU:0, one launch (start us, length us, event | category | flops | bytes accessed | tf_op | source)
XLA Modules:
  0.0 237.2 jit_solution(2243668392952579948)
XLA Ops:
  15.1 5.6 %all-gather.4.cloned.1.call-done = f32[2,128,1024]{2,1,0:T(8,128)} async-done(((f32[1,128,1024]{2,1,0:T(8,128)}), f32[2,128,1024]{2,1,0:T(8,128)}) %all-gather.4.cloned.1.call-update) | async-done | bytes 1048592 | tf_op jit(solution)/shard_map/all_gather | solution.py:147
  20.7 60.1 %while.47 = (s32[]{:T(128)}, bf16[64,1024]{1,0:T(8,128)(2,1)S(1)}, bf16[2,64,1024]{2,1,0:T(8,128)(2,1)S(1)}, bf16[2,70,1024]{2,1,0:T(8,128)(2,1)}, bf16[2,191,10...) while((s32[]{:T(128)}, bf16[64,1024]{1,0:T(8,128)(2,1)S(1)}, ...), condition=%wide.region_3.4_spmd, body=%wide.region_0.3_spmd.sunk | while | flops 125661312 | bytes 16984936 | solution.py:162
  20.8 10.1 %psum.30 = f32[64]{0:T(128)S(1)} all-reduce(f32[64]{0:T(128)S(1)} %fusion.164), channel_id=1, replica_groups=mesh['section'=2,'seq'=4,'chan'=4] {'chan'}, use_global_device_ids=true, to_apply=%region_2.2 | all-reduce | flops 64 | bytes 512 | tf_op jit(solution)/shard_map/while/body/eval_jaxpr/while/body/eval_jaxpr/psum | solution.py:59
  31.0 3.4 %collective-permute-start = (bf16[6,1024]{1,0:T(8,128)(2,1)S(1)}, bf16[6,1024]{1,0:T(8,128)(2,1)S(1)}, u32[]{:S(2)}, u32[]{:S(2)}) collective-permute-start(bf16[6,1024]{1,0:T(8,128)(2,1)S(1)} %slice.231), channel_id=1, source_target_pairs={{0,4},{4,8},{8,12},{1,5},{5,9},{9,13},{2,6},{6,10},{10,14},{3,7},{... | collective-permute-start | bytes 36872 | tf_op jit(solution)/shard_map/while/body/eval_jaxpr/while/body/eval_jaxpr/ppermute | solution.py:15
  37.8 3.4 %collective-permute-start.1 = (bf16[64,1024]{1,0:T(8,128)(2,1)S(1)}, bf16[64,1024]{1,0:T(8,128)(2,1)S(1)}, u32[]{:S(2)}, u32[]{:S(2)}) collective-permute-start(bf16[64,1024]{1,0:T(8,128)(2,1)S(1)} %slice_bitcast_fusion.13), channel_id=1, source_target_pairs={{0,4},{4,8},{8,12},{1,5},{5,9},{9,13},{2,6},{6,10},{10,14},{3,7},{... | collective-permute-start | bytes 393224 | tf_op jit(solution)/shard_map/while/body/eval_jaxpr/while/body/eval_jaxpr/ppermute | solution.py:15
  41.2 4.1 %collective-permute-start.2 = (bf16[63,1024]{1,0:T(8,128)(2,1)S(1)}, bf16[63,1024]{1,0:T(8,128)(2,1)S(1)}, u32[]{:S(2)}, u32[]{:S(2)}) collective-permute-start(bf16[63,1024]{1,0:T(8,128)(2,1)S(1)} %slice_bitcast_fusion.14), channel_id=1, source_target_pairs={{0,8},{4,12},{1,9},{5,13},{2,10},{6,14},{3,11},{7,15},{16,24},{20,... | collective-permute-start | bytes 387080 | tf_op jit(solution)/shard_map/while/body/eval_jaxpr/while/body/eval_jaxpr/ppermute | solution.py:15
  47.9 3.1 %fusion.168 = f32[1,64,1024]{2,0,1:T(1,128)S(1)} fusion(f32[128,1,1024]{2,1,0:T(1,128)S(1)} %broadcast_in_dim.132, bf16[1,191,1024]{2,1,0:T(8,128)(2,1)S(1)} %maximum_bitcast_fusion.7), kind=kOutput, calls=%fused_computation.5.clone.1 | convolution fusion | flops 100663296 | bytes 1177600 | tf_op jit(solution)/shard_map/while/body/eval_jaxpr/while/body/eval_jaxpr/conv_general_dilated | solution.py:23
  52.0 8.0 %psum.30 = f32[64]{0:T(128)S(1)} all-reduce(f32[64]{0:T(128)S(1)} %fusion.164), channel_id=1, replica_groups=mesh['section'=2,'seq'=4,'chan'=4] {'chan'}, use_global_device_ids=true, to_apply=%region_2.2 | all-reduce | flops 64 | bytes 512 | tf_op jit(solution)/shard_map/while/body/eval_jaxpr/while/body/eval_jaxpr/psum | solution.py:59
  65.7 5.7 %collective-permute-start.1 = (bf16[64,1024]{1,0:T(8,128)(2,1)S(1)}, bf16[64,1024]{1,0:T(8,128)(2,1)S(1)}, u32[]{:S(2)}, u32[]{:S(2)}) collective-permute-start(bf16[64,1024]{1,0:T(8,128)(2,1)S(1)} %slice_bitcast_fusion.13), channel_id=1, source_target_pairs={{0,4},{4,8},{8,12},{1,5},{5,9},{9,13},{2,6},{6,10},{10,14},{3,7},{... | collective-permute-start | bytes 393224 | tf_op jit(solution)/shard_map/while/body/eval_jaxpr/while/body/eval_jaxpr/ppermute | solution.py:15
  71.4 2.8 %collective-permute-start.2 = (bf16[63,1024]{1,0:T(8,128)(2,1)S(1)}, bf16[63,1024]{1,0:T(8,128)(2,1)S(1)}, u32[]{:S(2)}, u32[]{:S(2)}) collective-permute-start(bf16[63,1024]{1,0:T(8,128)(2,1)S(1)} %slice_bitcast_fusion.14), channel_id=1, source_target_pairs={{0,8},{4,12},{1,9},{5,13},{2,10},{6,14},{3,11},{7,15},{16,24},{20,... | collective-permute-start | bytes 387080 | tf_op jit(solution)/shard_map/while/body/eval_jaxpr/while/body/eval_jaxpr/ppermute | solution.py:15
  76.8 3.1 %fusion.168 = f32[1,64,1024]{2,0,1:T(1,128)S(1)} fusion(f32[128,1,1024]{2,1,0:T(1,128)S(1)} %broadcast_in_dim.132, bf16[1,191,1024]{2,1,0:T(8,128)(2,1)S(1)} %maximum_bitcast_fusion.7), kind=kOutput, calls=%fused_computation.5.clone.1 | convolution fusion | flops 100663296 | bytes 1177600 | tf_op jit(solution)/shard_map/while/body/eval_jaxpr/while/body/eval_jaxpr/conv_general_dilated | solution.py:23
  82.4 91.6 %while.48 = (s32[]{:T(128)}, bf16[64,1024]{1,0:T(8,128)(2,1)S(1)}, f32[2,151,1024]{2,1,0:T(8,128)}, f32[2,64]{1,0:T(2,128)S(1)}, f32[2,1024]{1,0:T(2,128)S(1)}, ...) while((s32[]{:T(128)}, bf16[64,1024]{1,0:T(8,128)(2,1)S(1)}, ...), condition=%wide.region_9.10_spmd, body=%wide.region_4.9_spmd.sunk | while | flops 268259520 | bytes 44115968 | solution.py:168
  88.7 3.1 %fusion.194 = f32[1,64,1024]{2,0,1:T(1,128)S(1)} fusion(f32[128,1,1024]{2,1,0:T(1,128)S(1)} %broadcast_in_dim.133, bf16[1,191,1024]{2,1,0:T(8,128)(2,1)S(1)} %constant_dynamic-slice_fusion.23), kind=kOutput, calls=%fused_computation.162.clone.1 | convolution fusion | flops 100663296 | bytes 1177600 | tf_op jit(solution)/shard_map/while/body/eval_jaxpr/while/body/eval_jaxpr/conv_general_dilated | solution.py:23
  96.4 5.0 %fusion.205 = f32[1,128,1024]{2,0,1:T(1,128)} fusion(bf16[64,1,1024]{2,0,1:T(8,128)(2,1)S(1)} %bitcast.315, bf16[1,191,1024]{2,1,0:T(8,128)(2,1)S(1)} %constant_dynamic-slice_fusion.23), kind=kOutput, calls=%fused_computation.89.clone.1 | convolution fusion | flops 16777216 | bytes 1046528 | tf_op jit(solution)/shard_map/while/body/eval_jaxpr/while/body/eval_jaxpr/conv_general_dilated | solution.py:23
  104.9 3.2 %fusion.196 = f32[1,64,1024]{2,0,1:T(1,128)S(1)} fusion(bf16[1,191,1024]{2,1,0:T(8,128)(2,1)S(1)} %maximum_bitcast_fusion.8, f32[1,128,1024]{2,1,0:T(8,128)S(1)} %constant_dynamic-slice_fusion.25), kind=kOutput, calls=%fused_computation.47.clone.1 | convolution fusion | flops 100663296 | bytes 1177600 | tf_op jit(solution)/shard_map/while/body/eval_jaxpr/while/body/eval_jaxpr/conv_general_dilated | solution.py:23
  111.1 4.3 %collective-permute-done.5 = bf16[6,3,1024]{2,0,1:T(8,128)(2,1)S(1)} collective-permute-done((bf16[6,3,1024]{2,0,1:T(8,128)(2,1)S(1)}, bf16[6,3,1024]{2,0,1:T(8,128)(2,1)S(1)}, u32[]{:S(2)}, u32[]{:S(2)}) %collective-permute-start.5) | collective-permute-done | bytes 36896 | tf_op jit(solution)/shard_map/while/body/eval_jaxpr/while/body/eval_jaxpr/ppermute | solution.py:15
  117.8 9.0 %psum.31 = f32[64]{0:T(128)S(1)} all-reduce(f32[64]{0:T(128)S(1)} %get-tuple-element.593), channel_id=1, replica_groups=mesh['section'=2,'seq'=4,'chan'=4] {'chan'}, use_global_device_ids=true, to_apply=%region_6.6 | all-reduce | flops 64 | bytes 512 | tf_op jit(solution)/shard_map/while/body/eval_jaxpr/while/body/eval_jaxpr/psum | solution.py:129
  134.8 3.1 %fusion.194 = f32[1,64,1024]{2,0,1:T(1,128)S(1)} fusion(f32[128,1,1024]{2,1,0:T(1,128)S(1)} %broadcast_in_dim.133, bf16[1,191,1024]{2,1,0:T(8,128)(2,1)S(1)} %constant_dynamic-slice_fusion.23), kind=kOutput, calls=%fused_computation.162.clone.1 | convolution fusion | flops 100663296 | bytes 1177600 | tf_op jit(solution)/shard_map/while/body/eval_jaxpr/while/body/eval_jaxpr/conv_general_dilated | solution.py:23
  142.5 5.0 %fusion.205 = f32[1,128,1024]{2,0,1:T(1,128)} fusion(bf16[64,1,1024]{2,0,1:T(8,128)(2,1)S(1)} %bitcast.315, bf16[1,191,1024]{2,1,0:T(8,128)(2,1)S(1)} %constant_dynamic-slice_fusion.23), kind=kOutput, calls=%fused_computation.89.clone.1 | convolution fusion | flops 16777216 | bytes 1046528 | tf_op jit(solution)/shard_map/while/body/eval_jaxpr/while/body/eval_jaxpr/conv_general_dilated | solution.py:23
  151.0 3.2 %fusion.196 = f32[1,64,1024]{2,0,1:T(1,128)S(1)} fusion(bf16[1,191,1024]{2,1,0:T(8,128)(2,1)S(1)} %maximum_bitcast_fusion.8, f32[1,128,1024]{2,1,0:T(8,128)S(1)} %constant_dynamic-slice_fusion.25), kind=kOutput, calls=%fused_computation.47.clone.1 | convolution fusion | flops 100663296 | bytes 1177600 | tf_op jit(solution)/shard_map/while/body/eval_jaxpr/while/body/eval_jaxpr/conv_general_dilated | solution.py:23
  157.1 4.8 %collective-permute-done.5 = bf16[6,3,1024]{2,0,1:T(8,128)(2,1)S(1)} collective-permute-done((bf16[6,3,1024]{2,0,1:T(8,128)(2,1)S(1)}, bf16[6,3,1024]{2,0,1:T(8,128)(2,1)S(1)}, u32[]{:S(2)}, u32[]{:S(2)}) %collective-permute-start.5) | collective-permute-done | bytes 36896 | tf_op jit(solution)/shard_map/while/body/eval_jaxpr/while/body/eval_jaxpr/ppermute | solution.py:15
  164.4 8.0 %psum.31 = f32[64]{0:T(128)S(1)} all-reduce(f32[64]{0:T(128)S(1)} %get-tuple-element.593), channel_id=1, replica_groups=mesh['section'=2,'seq'=4,'chan'=4] {'chan'}, use_global_device_ids=true, to_apply=%region_6.6 | all-reduce | flops 64 | bytes 512 | tf_op jit(solution)/shard_map/while/body/eval_jaxpr/while/body/eval_jaxpr/psum | solution.py:129
  174.1 10.3 %reduce-scatter.2.cloned.1.call-done = f32[1,151,1024]{2,1,0:T(8,128)} async-done(((f32[2,151,1024]{2,1,0:T(8,128)}), f32[1,151,1024]{2,1,0:T(8,128)}) %reduce-scatter.2.cloned.1.call-update) | async-done | bytes 618512 | tf_op jit(solution)/shard_map/reduce_scatter | solution.py:173
  184.5 43.7 %all-reduce.2.cloned.1.call-done = f32[1,151,1024]{2,1,0:T(8,128)} async-done(((f32[1,151,1024]{2,1,0:T(8,128)}), f32[1,151,1024]{2,1,0:T(8,128)}) %all-reduce.2.cloned.1.call-update) | async-done | bytes 618512 | tf_op jit(solution)/shard_map/psum | solution.py:174
  (291 shorter events, 70.7 us)
Async XLA Ops:
  6.5 14.1 %copy-start.13 = (pred[8,9]{0,1:T(8,128)(4,1)S(1)}, pred[8,9]{0,1:T(8,128)(4,1)}, u32[]{:S(2)}) copy-start(pred[8,9]{0,1:T(8,128)(4,1)} %constant.370) | copy-start | bytes 220
  6.5 8.5 %copy-start.11 = (bf16[2,64,1024]{2,1,0:T(8,128)(2,1)S(1)}, bf16[2,64,1024]{2,1,0:T(8,128)(2,1)}, u32[]{:S(2)}) copy-start(bf16[2,64,1024]{2,1,0:T(8,128)(2,1)} %param.10) | copy-start | bytes 786436
  6.5 8.5 %copy-start.12 = (bf16[2,64,1024]{2,1,0:T(8,128)(2,1)S(1)}, bf16[2,64,1024]{2,1,0:T(8,128)(2,1)}, u32[]{:S(2)}) copy-start(bf16[2,64,1024]{2,1,0:T(8,128)(2,1)} %param.11) | copy-start | bytes 786436
  6.5 14.1 %all-gather.4.cloned.1.call-start = ((), (), s32[]{:S(2)}) async-start(), calls=%async_computation.1 | async-start | bytes 1572864 | tf_op jit(solution)/shard_map/all_gather | solution.py:147
  7.3 177.2 %reduce-scatter.2.cloned.1.call-start = ((), (), s32[]{:S(2)}) async-start(), calls=%async_computation.2 | async-start | bytes 1867776 | tf_op jit(solution)/shard_map/reduce_scatter | solution.py:173
  31.0 5.9 %collective-permute-start = (bf16[6,1024]{1,0:T(8,128)(2,1)S(1)}, bf16[6,1024]{1,0:T(8,128)(2,1)S(1)}, u32[]{:S(2)}, u32[]{:S(2)}) collective-permute-start(bf16[6,1024]{1,0:T(8,128)(2,1)S(1)} %slice.231), channel_id=1, source_target_pairs={{0,4},{4,8},{8,12},{1,5},{5,9},{9,13},{2,6},{6,10},{10,14},{3,7},{... | collective-permute-start | bytes 36872 | tf_op jit(solution)/shard_map/while/body/eval_jaxpr/while/body/eval_jaxpr/ppermute | solution.py:15
  37.8 10.0 %collective-permute-start.1 = (bf16[64,1024]{1,0:T(8,128)(2,1)S(1)}, bf16[64,1024]{1,0:T(8,128)(2,1)S(1)}, u32[]{:S(2)}, u32[]{:S(2)}) collective-permute-start(bf16[64,1024]{1,0:T(8,128)(2,1)S(1)} %slice_bitcast_fusion.13), channel_id=1, source_target_pairs={{0,4},{4,8},{8,12},{1,5},{5,9},{9,13},{2,6},{6,10},{10,14},{3,7},{... | collective-permute-start | bytes 393224 | tf_op jit(solution)/shard_map/while/body/eval_jaxpr/while/body/eval_jaxpr/ppermute | solution.py:15
  41.2 6.6 %collective-permute-start.2 = (bf16[63,1024]{1,0:T(8,128)(2,1)S(1)}, bf16[63,1024]{1,0:T(8,128)(2,1)S(1)}, u32[]{:S(2)}, u32[]{:S(2)}) collective-permute-start(bf16[63,1024]{1,0:T(8,128)(2,1)S(1)} %slice_bitcast_fusion.14), channel_id=1, source_target_pairs={{0,8},{4,12},{1,9},{5,13},{2,10},{6,14},{3,11},{7,15},{16,24},{20,... | collective-permute-start | bytes 387080 | tf_op jit(solution)/shard_map/while/body/eval_jaxpr/while/body/eval_jaxpr/ppermute | solution.py:15
  46.5 4.5 %copy-start.10 = (bf16[2,70,1024]{2,1,0:T(8,128)(2,1)}, bf16[2,70,1024]{2,1,0:T(8,128)(2,1)S(1)}, u32[]{:S(2)}) copy-start(bf16[2,70,1024]{2,1,0:T(8,128)(2,1)S(1)} %constant_dynamic-update-slice_fusion.4) | copy-start | bytes 860164 | tf_op jit(solution)/shard_map/while/body/eval_jaxpr/while
  60.1 4.6 %collective-permute-start = (bf16[6,1024]{1,0:T(8,128)(2,1)S(1)}, bf16[6,1024]{1,0:T(8,128)(2,1)S(1)}, u32[]{:S(2)}, u32[]{:S(2)}) collective-permute-start(bf16[6,1024]{1,0:T(8,128)(2,1)S(1)} %slice.231), channel_id=1, source_target_pairs={{0,4},{4,8},{8,12},{1,5},{5,9},{9,13},{2,6},{6,10},{10,14},{3,7},{... | collective-permute-start | bytes 36872 | tf_op jit(solution)/shard_map/while/body/eval_jaxpr/while/body/eval_jaxpr/ppermute | solution.py:15
  65.7 11.0 %collective-permute-start.1 = (bf16[64,1024]{1,0:T(8,128)(2,1)S(1)}, bf16[64,1024]{1,0:T(8,128)(2,1)S(1)}, u32[]{:S(2)}, u32[]{:S(2)}) collective-permute-start(bf16[64,1024]{1,0:T(8,128)(2,1)S(1)} %slice_bitcast_fusion.13), channel_id=1, source_target_pairs={{0,4},{4,8},{8,12},{1,5},{5,9},{9,13},{2,6},{6,10},{10,14},{3,7},{... | collective-permute-start | bytes 393224 | tf_op jit(solution)/shard_map/while/body/eval_jaxpr/while/body/eval_jaxpr/ppermute | solution.py:15
  71.4 5.3 %collective-permute-start.2 = (bf16[63,1024]{1,0:T(8,128)(2,1)S(1)}, bf16[63,1024]{1,0:T(8,128)(2,1)S(1)}, u32[]{:S(2)}, u32[]{:S(2)}) collective-permute-start(bf16[63,1024]{1,0:T(8,128)(2,1)S(1)} %slice_bitcast_fusion.14), channel_id=1, source_target_pairs={{0,8},{4,12},{1,9},{5,13},{2,10},{6,14},{3,11},{7,15},{16,24},{20,... | collective-permute-start | bytes 387080 | tf_op jit(solution)/shard_map/while/body/eval_jaxpr/while/body/eval_jaxpr/ppermute | solution.py:15
  75.4 4.5 %copy-start.10 = (bf16[2,70,1024]{2,1,0:T(8,128)(2,1)}, bf16[2,70,1024]{2,1,0:T(8,128)(2,1)S(1)}, u32[]{:S(2)}) copy-start(bf16[2,70,1024]{2,1,0:T(8,128)(2,1)S(1)} %constant_dynamic-update-slice_fusion.4) | copy-start | bytes 860164 | tf_op jit(solution)/shard_map/while/body/eval_jaxpr/while
  82.4 3.6 %copy-start.5 = (bf16[2,64,1024]{2,1,0:T(8,128)(2,1)}, bf16[2,64,1024]{2,1,0:T(8,128)(2,1)S(1)}, u32[]{:S(2)}) copy-start(bf16[2,64,1024]{2,1,0:T(8,128)(2,1)S(1)} %get-tuple-element.689) | copy-start | bytes 786436 | tf_op jit(solution)/shard_map/while/body/eval_jaxpr/while
  83.4 18.0 %copy-start.1 = (bf16[1,70,1024]{2,1,0:T(8,128)(2,1)}, bf16[1,70,1024]{2,1,0:T(8,128)(2,1)S(1)}, u32[]{:S(2)}) copy-start(bf16[1,70,1024]{2,1,0:T(8,128)(2,1)S(1)} %constant_dynamic-slice_fusion.22) | copy-start | bytes 430084 | tf_op jit(solution)/shard_map/while/body/eval_jaxpr/while
  92.3 11.6 %collective-permute-start.4 = (bf16[64,1024]{1,0:T(8,128)(2,1)S(1)}, bf16[64,1024]{1,0:T(8,128)(2,1)}, u32[]{:S(2)}, u32[]{:S(2)}) collective-permute-start(bf16[64,1024]{1,0:T(8,128)(2,1)S(1)} %get-tuple-element.584), channel_id=1, source_target_pairs={{4,0},{8,4},{12,8},{5,1},{9,5},{13,9},{6,2},{10,6},{14,10},{7,3},{... | collective-permute-start | bytes 393224 | tf_op jit(solution)/shard_map/while/body/eval_jaxpr/while/body/eval_jaxpr/ppermute | solution.py:15
  93.6 10.3 %collective-permute-start.3 = (bf16[63,1024]{1,0:T(8,128)(2,1)S(1)}, bf16[63,1024]{1,0:T(8,128)(2,1)}, u32[]{:S(2)}, u32[]{:S(2)}) collective-permute-start(bf16[63,1024]{1,0:T(8,128)(2,1)S(1)} %bitcast.314), channel_id=1, source_target_pairs={{8,0},{12,4},{9,1},{13,5},{10,2},{14,6},{11,3},{15,7},{24,16},{28,... | collective-permute-start | bytes 387080 | tf_op jit(solution)/shard_map/while/body/eval_jaxpr/while/body/eval_jaxpr/ppermute | solution.py:15
  108.7 6.6 %collective-permute-start.5 = (bf16[6,3,1024]{2,0,1:T(8,128)(2,1)S(1)}, bf16[6,3,1024]{2,0,1:T(8,128)(2,1)S(1)}, u32[]{:S(2)}, u32[]{:S(2)}) collective-permute-start(bf16[6,3,1024]{2,0,1:T(8,128)(2,1)S(1)} %pad_maximum_fusion.5), channel_id=1, source_target_pairs={{4,0},{8,4},{12,8},{5,1},{9,5},{13,9},{6,2},{10,6},{14,10},{7,3},{... | collective-permute-start | bytes 110600 | tf_op jit(solution)/shard_map/while/body/eval_jaxpr/while/body/eval_jaxpr/ppermute | solution.py:15
  128.5 3.6 %copy-start.5 = (bf16[2,64,1024]{2,1,0:T(8,128)(2,1)}, bf16[2,64,1024]{2,1,0:T(8,128)(2,1)S(1)}, u32[]{:S(2)}) copy-start(bf16[2,64,1024]{2,1,0:T(8,128)(2,1)S(1)} %get-tuple-element.689) | copy-start | bytes 786436 | tf_op jit(solution)/shard_map/while/body/eval_jaxpr/while
  129.5 18.0 %copy-start.1 = (bf16[1,70,1024]{2,1,0:T(8,128)(2,1)}, bf16[1,70,1024]{2,1,0:T(8,128)(2,1)S(1)}, u32[]{:S(2)}) copy-start(bf16[1,70,1024]{2,1,0:T(8,128)(2,1)S(1)} %constant_dynamic-slice_fusion.22) | copy-start | bytes 430084 | tf_op jit(solution)/shard_map/while/body/eval_jaxpr/while
  138.4 11.6 %collective-permute-start.4 = (bf16[64,1024]{1,0:T(8,128)(2,1)S(1)}, bf16[64,1024]{1,0:T(8,128)(2,1)}, u32[]{:S(2)}, u32[]{:S(2)}) collective-permute-start(bf16[64,1024]{1,0:T(8,128)(2,1)S(1)} %get-tuple-element.584), channel_id=1, source_target_pairs={{4,0},{8,4},{12,8},{5,1},{9,5},{13,9},{6,2},{10,6},{14,10},{7,3},{... | collective-permute-start | bytes 393224 | tf_op jit(solution)/shard_map/while/body/eval_jaxpr/while/body/eval_jaxpr/ppermute | solution.py:15
  139.7 10.3 %collective-permute-start.3 = (bf16[63,1024]{1,0:T(8,128)(2,1)S(1)}, bf16[63,1024]{1,0:T(8,128)(2,1)}, u32[]{:S(2)}, u32[]{:S(2)}) collective-permute-start(bf16[63,1024]{1,0:T(8,128)(2,1)S(1)} %bitcast.314), channel_id=1, source_target_pairs={{8,0},{12,4},{9,1},{13,5},{10,2},{14,6},{11,3},{15,7},{24,16},{28,... | collective-permute-start | bytes 387080 | tf_op jit(solution)/shard_map/while/body/eval_jaxpr/while/body/eval_jaxpr/ppermute | solution.py:15
  154.8 7.1 %collective-permute-start.5 = (bf16[6,3,1024]{2,0,1:T(8,128)(2,1)S(1)}, bf16[6,3,1024]{2,0,1:T(8,128)(2,1)S(1)}, u32[]{:S(2)}, u32[]{:S(2)}) collective-permute-start(bf16[6,3,1024]{2,0,1:T(8,128)(2,1)S(1)} %pad_maximum_fusion.5), channel_id=1, source_target_pairs={{4,0},{8,4},{12,8},{5,1},{9,5},{13,9},{6,2},{10,6},{14,10},{7,3},{... | collective-permute-start | bytes 110600 | tf_op jit(solution)/shard_map/while/body/eval_jaxpr/while/body/eval_jaxpr/ppermute | solution.py:15
  174.1 54.1 %all-reduce.2.cloned.1.call-start = ((), (), s32[]{:S(2)}) async-start(), calls=%async_computation.3 | async-start | bytes 1245184 | tf_op jit(solution)/shard_map/psum | solution.py:174
  (15 other events, 25.5 us)
Sparse Core Ops, SparseCore 0:
  8.9 11.7 all-gather.3
  174.2 10.2 reduce-scatter.1
  186.8 41.2 all-reduce.1
where the time goes:
time: 238 us; the launch traced here: 237 us
  waiting for transfers between devices  72.1 us (30%)
  blocking collectives  41 us (17%)
  local copies, waits for them, and re-layouts  37.2 us (16%)
  matrix products  36.4 us (15%)
  starting transfers between devices  29.3 us (12%)
  between operations  13.2 us (6%)
  other arithmetic  6.36 us (3%)
    psum x1, waiting for transfers between devices, on_device(): return lax.psum(local_grads, 'seq')  43.7 us
    conv_general_dilated x32, matrix products, correlate(): lax.conv_general_dilated(signal[None], filters[:, None, :], (1,), 'VALID'...  36.4 us
    ppermute x12, starting transfers between devices, shifted(): return lax.ppermute(block, axis, route)  29.2 us
    psum x2, blocking collectives, forward_layer(): squares = lax.psum(jnp.sum(x_float * x_float, axis=1), 'chan')  18.1 us
    psum x2, blocking collectives, backward_layer(): lax.psum(jnp.sum(gain_row * d_normed * x_float, axis=1), 'chan') / D  16.9 us
    ppermute x12, waiting for transfers between devices, shifted(): return lax.ppermute(block, axis, route)  11.8 us
    reduce_scatter x1, waiting for transfers between devices, on_device(): lax.psum_scatter(grads_done, 'section', scatter_dimension=0, tiled=True)  10.3 us
    dynamic_slice x10, local copies, waits for them, and re-layouts, one_micro(): lax.scan(backward_pass, top_grad, (gathered, stored_all), reverse=True)  7.43 us
  transfers between devices with their start and end apart: 15, of which 7 were waited for; matrix products, arithmetic and copies ran while one was open for 11% of the time, Pallas kernels for 0%

commit v1 on v0

--- a/solution.py
+++ b/solution.py
@@ -1,6 +1,11 @@
+import functools
+
 import jax
 import jax.numpy as jnp
+import numpy as np
 from jax import lax
+from jax.experimental import pallas as pl
+from jax.experimental.pallas import tpu as pltpu
 from jax.sharding import PartitionSpec as P
 
 D = 4096
@@ -174,6 +179,443 @@
     return lax.psum(local_grads, "seq")
 
 
+F32, BF16 = jnp.float32, jnp.bfloat16
+PAD = 8
+CHUNK = 32
+
+
+def split(value):
+    high = value.astype(BF16)
+    return high, (value - high.astype(F32)).astype(BF16)
+
+
+def mm(a, b):
+    return jnp.dot(a, b, preferred_element_type=F32)
+
+
+def mm3(a_high, a_low, value):
+    high, low = split(value)
+    return mm(a_high, high) + (mm(a_high, low) + mm(a_low, high))
+
+
+def lane_sums(value):
+    high, low = split(value)
+    both = jnp.concatenate([high, low], axis=1)
+    ones = jnp.ones((16, both.shape[1]), BF16)
+    sums = lax.dot_general(ones, both, (((1,), (1,)), ((), ())), preferred_element_type=F32)
+    return sums[0:1]
+
+
+def as_columns(row, width):
+    return jnp.transpose(jnp.broadcast_to(row, (width, row.shape[1])))
+
+
+def spectrum_size(rows, taps):
+    return -(-(rows + taps) // 128) * 128
+
+
+def spectrum_tables(rows, taps):
+    size = spectrum_size(rows, taps)
+    angle = (2 * np.pi / size) * (np.arange(size // 2)[:, None] + 0.5) * np.arange(rows)[None]
+    forward = np.concatenate([np.cos(angle), -np.sin(angle)], axis=0)
+    inverse = (2.0 / size) * forward.T
+
+    def pair(table):
+        table = table.astype(np.float32)
+        high = table.astype(BF16)
+        low = (table - high.astype(np.float32)).astype(BF16)
+        return np.stack([high, low])
+
+    return pair(forward), pair(inverse)
+
+
+def channel_kernel(sizes, x_in, g_in, sf_in, lf_in, sk_in, ng_in, fw_in, iv_in, out,
+                   x_own, x_all, g_all, sf, lf, sk, ng, fw, iv,
+                   part0_out, part0, part_out, part, xf, scale, normed, query, key, value, mixed, m_hat,
+                   filtered, f_hat, d_fil, d_hat, d_str, d_nor, e_one, fresh, fresh_out,
+                   loc_sem, x_send, x_recv, f_send, f_recv, p0_send, p0_recv, p_send, p_recv, o_send, o_recv):
+    S, Q, C, M, R, W, KS, KL, D = sizes
+    T = Q * R
+    N = spectrum_size(T, KL)
+    H = N // 2
+    L = S
+    P_ALL = S * Q * C
+    s, q, c = lax.axis_index("section"), lax.axis_index("seq"), lax.axis_index("chan")
+    me = (s * Q + q) * C + c
+    lane = lambda slot: pl.ds(pl.multiple_of(slot * W, W), W)
+    rows_at = lambda seq: pl.ds(pl.multiple_of(seq * R, R), R)
+
+    def at(section, seq, chan):
+        return {"section": section, "seq": seq, "chan": chan}
+
+    def peer(offset):
+        p = lax.rem(me + offset, P_ALL)
+        return p, at(p // (Q * C), (p // C) % Q, p % C)
+
+    def remote(src, dst, send, recv, where):
+        return pltpu.make_async_remote_copy(src_ref=src, dst_ref=dst, send_sem=send, recv_sem=recv,
+                                            device_id=where, device_id_type=pl.DeviceIdType.MESH)
+
+    own = q * S + s
+    locals_ = [
+        (x_in, x_own), (x_in.at[:, :, lane(own)], x_all.at[:, rows_at(q), :]),
+        (g_in.at[:, :, lane(own)], g_all.at[:, rows_at(q), :]),
+        (sf_in.at[:, :, :, lane(own)], sf.at[pl.ds(s, 1)]), (lf_in.at[:, :, lane(own)], lf.at[pl.ds(s, 1)]),
+        (sk_in.at[:, lane(own)], sk.at[s]), (ng_in.at[:, lane(own)], ng.at[s]),
+        (fw_in, fw), (iv_in, iv),
+    ]
+    local_copies = [pltpu.make_async_copy(a, b, loc_sem.at[i]) for i, (a, b) in enumerate(locals_)]
+    for copy in local_copies:
+        copy.start()
+
+    barrier = pltpu.get_barrier_semaphore()
+
+    def greet(offset, carry):
+        pl.semaphore_signal(barrier, inc=1, device_id=peer(offset)[1], device_id_type=pl.DeviceIdType.MESH)
+        return carry
+
+    lax.fori_loop(1, P_ALL, greet, 0)
+
+    local_copies[0].wait()
+    for m in range(M):
+        total = None
+        for b in range(x_own.shape[2] // W):
+            piece = x_own[m, :, b * W:(b + 1) * W].astype(F32)
+            total = piece * piece if total is None else total + piece * piece
+        d_nor[m, 0:R, :] = total
+    gathered = jnp.concatenate([d_nor[m, 0:R, :] for m in range(M)], axis=0)
+    part0_out[...] = lane_sums(gathered)
+
+    pl.semaphore_wait(barrier, P_ALL - 1)
+
+    def p0_slot(seq, chan):
+        return seq * C + chan
+
+    def p0_copy(offset):
+        p = lax.rem(q * C + c + offset, Q * C)
+        return remote(part0_out, part0.at[q * C + c], p0_send.at[p], p0_recv.at[q * C + c], at(s, p // C, p % C))
+
+    def p0_start(offset, carry):
+        p0_copy(offset).start()
+        return carry
+
+    lax.fori_loop(1, Q * C, p0_start, 0)
+    x_copies, g_copies = [], []
+    for offset in range(1, Q):
+        to = lax.rem(q + offset, Q)
+        src_slot = to * S + s
+        x_copies.append(remote(x_in.at[:, :, lane(src_slot)], x_all.at[:, rows_at(q), :], x_send.at[0, offset], x_recv.at[0, offset], at(s, to, c)))
+        g_copies.append(remote(g_in.at[:, :, lane(src_slot)], g_all.at[:, rows_at(q), :], x_send.at[1, offset], x_recv.at[1, offset], at(s, to, c)))
+    for copy in x_copies:
+        copy.start()
+    mate = 1 - s
+    theirs = q * S + mate
+    f_copies = [
+        remote(src, dst, f_send.at[i], f_recv.at[i], at(mate, q, c))
+        for i, (src, dst) in enumerate([
+            (sf_in.at[:, :, :, lane(theirs)], sf.at[pl.ds(s, 1)]), (lf_in.at[:, :, lane(theirs)], lf.at[pl.ds(s, 1)]),
+            (sk_in.at[:, lane(theirs)], sk.at[s]), (ng_in.at[:, lane(theirs)], ng.at[s]),
+        ])
+    ]
+    for copy in f_copies:
+        copy.start()
+    for copy in g_copies:
+        copy.start()
+
+    for l in range(L):
+        for m in range(M):
+            normed[l, m, 0:PAD, :] = jnp.zeros((PAD, W), F32)
+    for i in range(3):
+        for m in range(M):
+            d_str[i, m, T:T + PAD, :] = jnp.zeros((PAD, W), F32)
+    for copy in local_copies[1:]:
+        copy.wait()
+    for copy in f_copies:
+        copy.wait()
+    for l in range(L):
+        f_hat[l] = mm3(fw[0, :, 0:KL], fw[1, :, 0:KL], lf[l])
+        f_hat[l, 0:H, :] = f_hat[l, 0:H, :] + sk[l]
+
+    def p0_wait(offset, carry):
+        p = lax.rem(q * C + c + offset, Q * C)
+        remote(part0_out, part0.at[p], p0_send.at[p], p0_recv.at[p], at(s, p // C, p % C)).wait_recv()
+        return carry
+
+    part0[q * C + c] = part0_out[...]
+    lax.fori_loop(1, Q * C, p0_wait, 0)
+    for seq in range(Q):
+        row = part0[seq * C]
+        for chan in range(1, C):
+            row = row + part0[seq * C + chan]
+        columns = as_columns(lax.rsqrt(row / D + EPSILON), W)
+        for m in range(M):
+            scale[0, m, seq * R:(seq + 1) * R, :] = columns[m * R:(m + 1) * R]
+    for copy in x_copies:
+        copy.wait_recv()
+    for m in range(M):
+        for t in range(0, T, R):
+            xf[0, m, t:t + R, :] = x_all[m, t:t + R, :].astype(F32)
+
+    def chunks(body):
+        def step(i, carry):
+            body(pl.multiple_of(i * CHUNK, CHUNK))
+            return carry
+
+        lax.fori_loop(0, T // CHUNK, step, 0)
+
+    def rounded(v):
+        return v.astype(BF16).astype(F32)
+
+    def forward(l):
+        gain = ng[l]
+        for m in range(M):
+            def norm_chunk(t):
+                v = xf[l, m, pl.ds(t, CHUNK), :] * scale[l, m, pl.ds(t, CHUNK), :] * gain
+                normed[l, m, pl.ds(t + PAD, CHUNK), :] = rounded(v)
+
+            chunks(norm_chunk)
+        taps = [[sf[l, i, j:j + 1, :] for j in range(KS)] for i in range(3)]
+        for m in range(M):
+            def short_chunk(t):
+                sums = [None] * 3
+                for j in range(KS):
+                    shifted_rows = normed[l, m, pl.ds(t + PAD - j, CHUNK), :]
+                    for i in range(3):
+                        term = taps[i][j] * shifted_rows
+                        sums[i] = term if sums[i] is None else sums[i] + term
+                query[l, m, pl.ds(t, CHUNK), :] = sums[0]
+                key[l, m, pl.ds(t, CHUNK), :] = sums[1]
+                value[l, m, pl.ds(t, CHUNK), :] = sums[2]
+                mixed[pl.ds(t, CHUNK), m * W:(m + 1) * W] = (sums[1] * sums[2]).astype(BF16)
+
+            chunks(short_chunk)
+        m_hat[l] = mm(fw[0], mixed[...]) + mm(fw[1], mixed[...])
+        pieces = []
+        for m in range(M):
+            fr, fi = f_hat[l, 0:H, :], f_hat[l, H:N, :]
+            mr, mi = m_hat[l, 0:H, m * W:(m + 1) * W], m_hat[l, H:N, m * W:(m + 1) * W]
+            pieces.append(jnp.concatenate([fr * mr - fi * mi, fr * mi + fi * mr], axis=0))
+        result = mm3(iv[0], iv[1], jnp.concatenate(pieces, axis=1))
+        for m in range(M):
+            filtered[l, m] = result[:, m * W:(m + 1) * W]
+
+    def exchange(stage, rows_of):
+        part_out[stage] = jnp.concatenate([lane_sums(rows_of(m)) for m in range(M)], axis=1)
+
+        def send(offset, carry):
+            p, where = peer(offset)
+            remote(part_out.at[stage], part.at[stage, me], p_send.at[stage, p], p_recv.at[stage, me], where).start()
+            return carry
+
+        lax.fori_loop(1, P_ALL, send, 0)
+
+    def exchanged(stage):
+        part[stage, me] = part_out[stage]
+
+        def wait(offset, carry):
+            p, where = peer(offset)
+            remote(part_out.at[stage], part.at[stage, p], p_send.at[stage, p], p_recv.at[stage, p], where).wait_recv()
+            return carry
+
+        lax.fori_loop(1, P_ALL, wait, 0)
+        rows = [part[stage, p] for p in range(P_ALL)]
+        while len(rows) > 1:
+            rows = [a + b for a, b in zip(rows[::2], rows[1::2])] + ([rows[-1]] if len(rows) % 2 else [])
+        return rows[0]
+
+    for l in range(L):
+        forward(l)
+        if l < L - 1:
+            for m in range(M):
+                xf[l + 1, m] = rounded(xf[l, m] + query[l, m] * filtered[l, m])
+            exchange(l, lambda m: xf[l + 1, m] * xf[l + 1, m])
+            root = lax.rsqrt(exchanged(l) / D + EPSILON)
+            for m in range(M):
+                scale[l + 1, m] = as_columns(root[:, m * T:(m + 1) * T], W)
+
+    for copy in g_copies:
+        copy.wait_recv()
+
+    def send_rows(l, part_index, low, high):
+        for seq in range(Q):
+            here = jnp.logical_and(s == l, q == seq)
+
+            @pl.when(here)
+            def _():
+                out[low:high, lane(own)] = fresh_out[l, low:high, :]
+
+            @pl.when(jnp.logical_not(here))
+            def _():
+                remote(fresh_out.at[l, low:high, :], out.at[low:high, lane(own)], o_send.at[l, part_index, seq],
+                       o_recv.at[part_index, own], at(l, seq, c)).start()
+
+    rows_total = 3 * KS + KL + 2
+    early_low = -(-3 * KS // 16) * 16
+    early_high = (3 * KS + KL) // 16 * 16
+    late_high = fresh_out.shape[1]
+    spans = [(early_low, early_high), (0, early_low), (early_high, late_high)]
+    stages = L - 1
+    for l in reversed(range(L)):
+        top = l == L - 1
+        for m in range(M):
+            e = g_all[m].astype(F32) if top else e_one[m]
+            d_str[0, m, 0:T, :] = rounded(e * filtered[l, m])
+            d_fil[:, m * W:(m + 1) * W] = (e * query[l, m]).astype(BF16)
+        d_hat[...] = mm(fw[0], d_fil[...]) + mm(fw[1], d_fil[...])
+
+        def long_gradient():
+            re, im = None, None
+            for m in range(M):
+                dr, di = d_hat[0:H, m * W:(m + 1) * W], d_hat[H:N, m * W:(m + 1) * W]
+                mr, mi = m_hat[l, 0:H, m * W:(m + 1) * W], m_hat[l, H:N, m * W:(m + 1) * W]
+                a, b = dr * mr + di * mi, di * mr - dr * mi
+                re, im = (a, b) if re is None else (re + a, im + b)
+            taps_grad = mm3(iv[0, 0:KL, :], iv[1, 0:KL, :], jnp.concatenate([re, im], axis=0))
+            fresh[3 * KS:3 * KS + KL, :] = taps_grad
+            fresh[3 * KS + KL:3 * KS + KL + 1, :] = taps_grad[0:1]
+            fresh_out[l, early_low:early_high, :] = fresh[early_low:early_high, :].astype(BF16)
+            send_rows(l, 0, early_low, early_high)
+
+        if not top:
+            long_gradient()
+        pieces = []
+        for m in range(M):
+            fr, fi = f_hat[l, 0:H, :], f_hat[l, H:N, :]
+            dr, di = d_hat[0:H, m * W:(m + 1) * W], d_hat[H:N, m * W:(m + 1) * W]
+            pieces.append(jnp.concatenate([fr * dr + fi * di, fr * di - fi * dr], axis=0))
+        d_mix = mm3(iv[0], iv[1], jnp.concatenate(pieces, axis=1))
+        for m in range(M):
+            d_mix_m = d_mix[:, m * W:(m + 1) * W]
+            d_str[1, m, 0:T, :] = rounded(d_mix_m * value[l, m])
+            d_str[2, m, 0:T, :] = rounded(d_mix_m * key[l, m])
+        taps = [[sf[l, i, j:j + 1, :] for j in range(KS)] for i in range(3)]
+        for m in range(M):
+            def normed_chunk(t):
+                total = None
+                for i in range(3):
+                    for j in range(KS):
+                        term = taps[i][j] * d_str[i, m, pl.ds(t + j, CHUNK), :]
+                        total = term if total is None else total + term
+                d_nor[m, pl.ds(t, CHUNK), :] = total
+
+            chunks(normed_chunk)
+        gain = ng[l]
+        if l > 0:
+            exchange(stages, lambda m: gain * d_nor[m] * xf[l, m])
+        if top:
+            long_gradient()
+        fold = lambda v: jnp.sum(v.reshape(CHUNK // 8, 8, W), axis=0)
+        zeros = tuple(jnp.zeros((8, W), F32) for _ in range(3 * KS + 1))
+
+        def grad_chunk(i, carry):
+            t = pl.multiple_of(i * CHUNK, CHUNK)
+            sums = list(carry)
+            for m in range(M):
+                streams = [d_str[k, m, pl.ds(t, CHUNK), :] for k in range(3)]
+                for j in range(KS):
+                    shifted_rows = normed[l, m, pl.ds(t + PAD - j, CHUNK), :]
+                    for k in range(3):
+                        sums[k * KS + j] = sums[k * KS + j] + fold(streams[k] * shifted_rows)
+                gain_terms = d_nor[m, pl.ds(t, CHUNK), :] * xf[l, m, pl.ds(t, CHUNK), :] * scale[l, m, pl.ds(t, CHUNK), :]
+                sums[3 * KS] = sums[3 * KS] + fold(gain_terms)
+            return tuple(sums)
+
+        sums = lax.fori_loop(0, T // CHUNK, grad_chunk, zeros)
+        for row in range(3 * KS):
+            fresh[row:row + 1, :] = jnp.sum(sums[row], axis=0, keepdims=True)
+        fresh[rows_total - 1:rows_total, :] = jnp.sum(sums[3 * KS], axis=0, keepdims=True)
+        for index in (1, 2):
+            low, high = spans[index]
+            fresh_out[l, low:high, :] = fresh[low:high, :].astype(BF16)
+            send_rows(l, index, low, high)
+        if l > 0:
+            norm_row = exchanged(stages) / D
+            for m in range(M):
+                term = as_columns(norm_row[:, m * T:(m + 1) * T], W)
+                r = scale[l, m]
+                e_one[m] = rounded(g_all[m].astype(F32) + r * gain * d_nor[m] - xf[l, m] * (r * r * r) * term)
+
+    for seq in range(Q):
+        for sec in range(S):
+            slot = seq * S + sec
+            here = jnp.logical_and(s == sec, q == seq)
+
+            @pl.when(jnp.logical_not(here))
+            def _():
+                for index, (low, high) in enumerate(spans):
+                    remote(fresh_out.at[0, low:high, :], out.at[low:high, slot * W:(slot + 1) * W], o_send.at[0, index, 0],
+                           o_recv.at[index, slot], at(s, q, c)).wait_recv()
+    for l in range(L):
+        for seq in range(Q):
+            here = jnp.logical_and(s == l, q == seq)
+
+            @pl.when(jnp.logical_not(here))
+            def _():
+                for index, (low, high) in enumerate(spans):
+                    remote(fresh_out.at[l, low:high, :], out.at[low:high, lane(own)], o_send.at[l, index, seq],
+                           o_recv.at[index, own], at(l, seq, c)).wait_send()
+    for copy in x_copies + g_copies:
+        copy.wait_send()
+
+    def p0_sent(offset, carry):
+        p0_copy(offset).wait_send()
+        return carry
+
+    lax.fori_loop(1, Q * C, p0_sent, 0)
+    for stage in range(L):
+        def sent(offset, carry):
+            p, where = peer(offset)
+            remote(part_out.at[stage], part.at[stage, me], p_send.at[stage, p], p_recv.at[stage, me], where).wait_send()
+            return carry
+
+        lax.fori_loop(1, P_ALL, sent, 0)
+
+
+def kernel_fits(mesh, args):
+    x, sf, lf = args[0], args[2], args[3]
+    S, Q = mesh.shape["section"], mesh.shape["seq"]
+    width = x.shape[2] // (S * Q)
+    rows = Q * x.shape[1]
+    return (S == 2 and sf.shape[0] == 1 and width * S * Q == x.shape[2] and width == 128
+            and x.shape[1] % CHUNK == 0 and x.shape[0] * x.shape[1] == 128 and sf.shape[2] <= PAD
+            and lf.shape[1] % 128 == 0 and lf.shape[1] <= rows)
+
+
+def by_channels(mesh, x, g, sf, lf, sk, ng):
+    S, Q, C = mesh.shape["section"], mesh.shape["seq"], mesh.shape["chan"]
+    M, R, channels = x.shape
+    KS, KL = sf.shape[2], lf.shape[1]
+    W, T, L, G = channels // (S * Q), Q * R, S, S * Q * C
+    N = spectrum_size(T, KL)
+    fw, iv = spectrum_tables(T, KL)
+    rows_total = 3 * KS + KL + 2
+    rows_out = -(-rows_total // 16) * 16
+    V, dma = pltpu.VMEM, pltpu.SemaphoreType.DMA
+    sizes = (S, Q, C, M, R, W, KS, KL, D)
+    big = lambda: V((L, M, T, W), F32)
+    spans = 3
+    result = pl.pallas_call(
+        functools.partial(channel_kernel, sizes),
+        out_shape=jax.ShapeDtypeStruct((rows_out, channels), BF16),
+        in_specs=[pl.BlockSpec(memory_space=pl.ANY)] * 8,
+        out_specs=pl.BlockSpec(memory_space=pltpu.VMEM),
+        scratch_shapes=[
+            V((M, R, channels), BF16), V((M, T, W), BF16), V((M, T, W), BF16),
+            V((L, 3, KS, W), F32), V((L, KL, W), F32), V((L, 1, W), F32), V((L, 1, W), F32),
+            V(fw.shape, BF16), V(iv.shape, BF16),
+            V((1, M * R), F32), V((Q * C, 1, M * R), F32), V((L, 1, M * T), F32), V((L, G, 1, M * T), F32),
+            big(), big(), V((L, M, PAD + T, W), F32), big(), big(), big(),
+            V((T, M * W), BF16), V((L, N, M * W), F32), big(), V((L, N, W), F32),
+            V((T, M * W), BF16), V((N, M * W), F32), V((3, M, T + PAD, W), F32), V((M, T, W), F32),
+            V((M, T, W), F32), V((rows_out, W), F32), V((L, rows_out, W), BF16),
+            dma((9,)), dma((2, Q)), dma((2, Q)), dma((4,)), dma((4,)), dma((Q * C,)), dma((Q * C,)),
+            dma((L, G)), dma((L, G)), dma((L, spans, Q)), dma((spans, S * Q)),
+        ],
+        compiler_params=pltpu.CompilerParams(collective_id=0, has_side_effects=True, vmem_limit_bytes=40 * 1024 * 1024),
+    )(x, g, sf, lf, sk, ng, jnp.asarray(fw), jnp.asarray(iv))
+    return result[:rows_total].astype(F32)[None]
+
+
 def solution(mesh):
     placed = (
         P(None, "seq", "chan"),
@@ -183,6 +625,12 @@
         P("section", "chan"),
         P("section", "chan"),
     )
+
+    def body(*args):
+        if kernel_fits(mesh, args):
+            return by_channels(mesh, *args)
+        return on_device(*args)
+
     return jax.shard_map(
-        on_device, mesh=mesh, in_specs=placed, out_specs=P("section", None, "chan"), check_vma=False
-    )
+        body, mesh=mesh, in_specs=placed, out_specs=P("section", None, "chan"), check_vma=False
+    )

time: 238 us -> 46.6 us (0.20)
  waiting for transfers between devices: 72.1 us -> 0 us
  blocking collectives: 41 us -> 0 us
  Pallas kernels: 0 us -> 38.9 us
  matrix products: 36.4 us -> 0 us
  local copies, waits for them, and re-layouts: 37.2 us -> 7.33 us
  starting transfers between devices: 29.3 us -> 0 us
  between operations: 13.2 us -> 0.05 us
  other arithmetic: 6.36 us -> 0.05 us
    psum x1 -> x0, waiting for transfers between devices: 43.7 us -> none  [on_device(): return lax.psum(local_grads, 'seq')]
    pallas_call x0 -> x1, Pallas kernels: none -> 38.9 us  [by_channels(): pl.pallas_call(functools.partial(channel_kernel, sizes), out_shape=jax.Sh...]
    conv_general_dilated x32 -> x0, matrix products: 36.4 us -> none  [correlate(): lax.conv_general_dilated(signal[None], filters[:, None, :], (1,), 'VALID'...]
    psum x4 -> x0, blocking collectives: 35 us -> none  [the longest x2 18.1 us: forward_layer(): squares = lax.psum(jnp.sum(x_float * x_float, axis=1), 'chan')]
    ppermute x12 -> x0, starting transfers between devices: 29.2 us -> none  [shifted(): return lax.ppermute(block, axis, route)]
    ppermute x12 -> x0, waiting for transfers between devices: 11.8 us -> none  [shifted(): return lax.ppermute(block, axis, route)]
    reduce_scatter x1 -> x0, waiting for transfers between devices: 10.3 us -> none  [on_device(): lax.psum_scatter(grads_done, 'section', scatter_dimension=0, tiled=True)]
    dynamic_slice x20 -> x0, local copies, waits for them, and re-layouts: 7.6 us -> none  [the longest x10 7.43 us: one_micro(): lax.scan(backward_pass, top_grad, (gathered, stored_all), reverse=True)]
  transfers between devices with their start and end apart: 15 -> 0, of which waited for: 7 -> 0; matrix products, arithmetic and copies ran while one was open for 11% -> 0% of each run, Pallas kernels for 0% -> 0%
where the time goes in v1:
time: 46.6 us; the launch traced here: 46.3 us
  Pallas kernels  38.9 us (83%)
  local copies, waits for them, and re-layouts  7.33 us (16%)
    pallas_call x1, Pallas kernels, by_channels(): pl.pallas_call(functools.partial(channel_kernel, sizes), out_shape=jax.Sh...  38.9 us
    unnamed x15, local copies, waits for them, and re-layouts  5.87 us
    broadcast_in_dim x1, local copies, waits for them, and re-layouts, by_channels(): return result[:rows_total].astype(F32)[None]  1.46 us

profile of v1, /device:TPU:0, one launch (start us, length us, event | category | flops | bytes accessed | tf_op | source)
XLA Modules:
  0.0 46.3 jit_solution(8431085548894025116)
XLA Ops:
  0.0 0.0 copy-start.6
  0.0 0.0 copy-start.5
  0.0 0.9 %copy.9.sf_in = f32[1,3,7,1024]{3,2,1,0:T(8,128)S(1)} copy(f32[1,3,7,1024]{3,0,2,1:T(1,128)} %param.10) | data formatting | bytes 172032 | tf_op args[2]
  0.9 0.0 copy-done.6
  1.0 0.0 copy-done.5
  1.0 0.0 copy-start
  1.0 1.0 %copy-done = f32[1,128,1024]{2,1,0:T(8,128)S(1)} copy-done((f32[1,128,1024]{2,1,0:T(8,128)S(1)}, f32[1,128,1024]{2,1,0:T(8,128)}, u32[]{:S(2)}) %copy-start) | copy-done | bytes 524312
  2.0 0.0 copy-start.1
  2.0 1.0 %copy-done.1 = bf16[2,256,384]{2,1,0:T(8,128)(2,1)S(1)} copy-done((bf16[2,256,384]{2,1,0:T(8,128)(2,1)S(1)}, bf16[2,256,384]{2,1,0:T(8,128)(2,1)}, u32[]{:S(2)}) %copy-start.1) | copy-done | bytes 393240
  3.0 0.0 copy-start.2
  3.0 1.0 %copy-done.2 = bf16[2,384,256]{2,1,0:T(8,128)(2,1)S(1)} copy-done((bf16[2,384,256]{2,1,0:T(8,128)(2,1)S(1)}, bf16[2,384,256]{2,1,0:T(8,128)(2,1)}, u32[]{:S(2)}) %copy-start.2) | copy-done | bytes 393240
  4.0 0.0 copy-start.3
  4.0 0.9 %copy-done.3 = bf16[2,64,1024]{2,1,0:T(8,128)(2,1)S(1)} copy-done((bf16[2,64,1024]{2,1,0:T(8,128)(2,1)S(1)}, bf16[2,64,1024]{2,1,0:T(8,128)(2,1)}, u32[]{:S(2)}) %copy-start.3) | copy-done | bytes 262168
  5.0 0.0 copy-start.4
  5.0 0.9 %copy-done.4 = bf16[2,64,1024]{2,1,0:T(8,128)(2,1)S(1)} copy-done((bf16[2,64,1024]{2,1,0:T(8,128)(2,1)S(1)}, bf16[2,64,1024]{2,1,0:T(8,128)(2,1)}, u32[]{:S(2)}) %copy-start.4) | copy-done | bytes 262168
  5.9 38.9 %shard_map.82 = bf16[160,1024]{1,0:T(8,128)(2,1)S(1)} custom-call(bf16[2,64,1024]{2,1,0:T(8,128)(2,1)S(1)} %copy-done.3, bf16[2,64,1024]{2,1,0:T(8,128)(2,1)S(1)} %copy-done.4, f32[1,3,7,1024]{3,2,1,0:T(8,128)S(1)} %copy.9.sf_in, f32[1,128,1024]{2,1,0:T(8,128)S(1)} %copy-done, f32[1,1024]{1,0:T(1,128)S(1)} %copy-done.5, f32[1,1024]{1,0:T(1,128)S(1)} %copy-done.6, ...), custom_call_target="tpu_custom_call" | custom-call | tf_op jit(solution)/shard_map/pallas_call | solution.py:597
  44.8 0.1 bitcast_convert_fusion
  44.8 1.5 %copy.10 = f32[1,151,1024]{2,0,1:T(1,128)} copy(f32[1,151,1024]{2,1,0:T(8,128)S(1)} %bitcast_convert_fusion) | data formatting | bytes 1236992 | tf_op jit(solution)/shard_map/broadcast_in_dim | solution.py:616
Async XLA Ops:
  0.0 0.9 %copy-start.6 = (f32[1,1024]{1,0:T(1,128)S(1)}, f32[1,1024]{1,0:T(1,128)}, u32[]{:S(2)}) copy-start(f32[1,1024]{1,0:T(1,128)} %ng_in.1) | copy-start | bytes 12292
  0.0 1.0 %copy-start.5 = (f32[1,1024]{1,0:T(1,128)S(1)}, f32[1,1024]{1,0:T(1,128)}, u32[]{:S(2)}) copy-start(f32[1,1024]{1,0:T(1,128)} %sk_in.1) | copy-start | bytes 12292
  1.0 1.0 %copy-start = (f32[1,128,1024]{2,1,0:T(8,128)S(1)}, f32[1,128,1024]{2,1,0:T(8,128)}, u32[]{:S(2)}) copy-start(f32[1,128,1024]{2,1,0:T(8,128)} %lf_in.1) | copy-start | bytes 1572868
  2.0 1.0 %copy-start.1 = (bf16[2,256,384]{2,1,0:T(8,128)(2,1)S(1)}, bf16[2,256,384]{2,1,0:T(8,128)(2,1)}, u32[]{:S(2)}) copy-start(bf16[2,256,384]{2,1,0:T(8,128)(2,1)} %constant.5.clone.iv_in) | copy-start | bytes 1179652
  3.0 1.0 %copy-start.2 = (bf16[2,384,256]{2,1,0:T(8,128)(2,1)S(1)}, bf16[2,384,256]{2,1,0:T(8,128)(2,1)}, u32[]{:S(2)}) copy-start(bf16[2,384,256]{2,1,0:T(8,128)(2,1)} %constant.4.clone.fw_in) | copy-start | bytes 1179652
  4.0 0.9 %copy-start.3 = (bf16[2,64,1024]{2,1,0:T(8,128)(2,1)S(1)}, bf16[2,64,1024]{2,1,0:T(8,128)(2,1)}, u32[]{:S(2)}) copy-start(bf16[2,64,1024]{2,1,0:T(8,128)(2,1)} %x_in.1) | copy-start | bytes 786436
  5.0 0.9 %copy-start.4 = (bf16[2,64,1024]{2,1,0:T(8,128)(2,1)S(1)}, bf16[2,64,1024]{2,1,0:T(8,128)(2,1)}, u32[]{:S(2)}) copy-start(bf16[2,64,1024]{2,1,0:T(8,128)(2,1)} %g_in.1) | copy-start | bytes 786436

commit v2 on v1

--- a/solution.py
+++ b/solution.py
@@ -232,7 +232,7 @@
 def channel_kernel(sizes, x_in, g_in, sf_in, lf_in, sk_in, ng_in, fw_in, iv_in, out,
                    x_own, x_all, g_all, sf, lf, sk, ng, fw, iv,
                    part0_out, part0, part_out, part, xf, scale, normed, query, key, value, mixed, m_hat,
-                   filtered, f_hat, d_fil, d_hat, d_str, d_nor, e_one, fresh, fresh_out,
+                   filtered, f_hat, d_fil, d_hat, d_str, d_nor, e_one, fresh, fresh_out, arrived,
                    loc_sem, x_send, x_recv, f_send, f_recv, p0_send, p0_recv, p_send, p_recv, o_send, o_recv):
     S, Q, C, M, R, W, KS, KL, D = sizes
     T = Q * R
@@ -260,7 +260,7 @@
     locals_ = [
         (x_in, x_own), (x_in.at[:, :, lane(own)], x_all.at[:, rows_at(q), :]),
         (g_in.at[:, :, lane(own)], g_all.at[:, rows_at(q), :]),
-        (sf_in.at[:, :, :, lane(own)], sf.at[pl.ds(s, 1)]), (lf_in.at[:, :, lane(own)], lf.at[pl.ds(s, 1)]),
+        (sf_in.at[:, :, lane(own)], sf.at[s]), (lf_in.at[:, :, lane(own)], lf.at[pl.ds(s, 1)]),
         (sk_in.at[:, lane(own)], sk.at[s]), (ng_in.at[:, lane(own)], ng.at[s]),
         (fw_in, fw), (iv_in, iv),
     ]
@@ -313,7 +313,7 @@
     f_copies = [
         remote(src, dst, f_send.at[i], f_recv.at[i], at(mate, q, c))
         for i, (src, dst) in enumerate([
-            (sf_in.at[:, :, :, lane(theirs)], sf.at[pl.ds(s, 1)]), (lf_in.at[:, :, lane(theirs)], lf.at[pl.ds(s, 1)]),
+            (sf_in.at[:, :, lane(theirs)], sf.at[s]), (lf_in.at[:, :, lane(theirs)], lf.at[pl.ds(s, 1)]),
             (sk_in.at[:, lane(theirs)], sk.at[s]), (ng_in.at[:, lane(theirs)], ng.at[s]),
         ])
     ]
@@ -374,7 +374,7 @@
                 normed[l, m, pl.ds(t + PAD, CHUNK), :] = rounded(v)
 
             chunks(norm_chunk)
-        taps = [[sf[l, i, j:j + 1, :] for j in range(KS)] for i in range(3)]
+        taps = [[sf[l, i * KS + j] for j in range(KS)] for i in range(3)]
         for m in range(M):
             def short_chunk(t):
                 sums = [None] * 3
@@ -436,20 +436,26 @@
     for copy in g_copies:
         copy.wait_recv()
 
+    slots = S * Q
+    rows_total = 3 * KS + KL + 2
+
+    def place(slot, low, high, values):
+        high = min(high, rows_total)
+        out[pl.ds(low * slots + slot, high - low, stride=slots), :] = values[0:high - low]
+
     def send_rows(l, part_index, low, high):
         for seq in range(Q):
             here = jnp.logical_and(s == l, q == seq)
 
             @pl.when(here)
             def _():
-                out[low:high, lane(own)] = fresh_out[l, low:high, :]
+                place(own, low, high, fresh[low:high, :])
 
             @pl.when(jnp.logical_not(here))
             def _():
-                remote(fresh_out.at[l, low:high, :], out.at[low:high, lane(own)], o_send.at[l, part_index, seq],
+                remote(fresh_out.at[l, low:high, :], arrived.at[own, low:high, :], o_send.at[l, part_index, seq],
                        o_recv.at[part_index, own], at(l, seq, c)).start()
 
-    rows_total = 3 * KS + KL + 2
     early_low = -(-3 * KS // 16) * 16
     early_high = (3 * KS + KL) // 16 * 16
     late_high = fresh_out.shape[1]
@@ -488,7 +494,7 @@
             d_mix_m = d_mix[:, m * W:(m + 1) * W]
             d_str[1, m, 0:T, :] = rounded(d_mix_m * value[l, m])
             d_str[2, m, 0:T, :] = rounded(d_mix_m * key[l, m])
-        taps = [[sf[l, i, j:j + 1, :] for j in range(KS)] for i in range(3)]
+        taps = [[sf[l, i * KS + j] for j in range(KS)] for i in range(3)]
         for m in range(M):
             def normed_chunk(t):
                 total = None
@@ -535,24 +541,21 @@
                 r = scale[l, m]
                 e_one[m] = rounded(g_all[m].astype(F32) + r * gain * d_nor[m] - xf[l, m] * (r * r * r) * term)
 
-    for seq in range(Q):
-        for sec in range(S):
-            slot = seq * S + sec
-            here = jnp.logical_and(s == sec, q == seq)
+    for index, (low, high) in enumerate(spans):
+        for slot in range(slots):
+            @pl.when(own != slot)
+            def _():
+                remote(fresh_out.at[0, low:high, :], arrived.at[slot, low:high, :], o_send.at[0, index, 0],
+                       o_recv.at[index, slot], at(s, q, c)).wait_recv()
+                place(slot, low, high, arrived[slot, low:high, :].astype(F32))
+    for l in range(L):
+        for seq in range(Q):
+            here = jnp.logical_and(s == l, q == seq)
 
             @pl.when(jnp.logical_not(here))
             def _():
                 for index, (low, high) in enumerate(spans):
-                    remote(fresh_out.at[0, low:high, :], out.at[low:high, slot * W:(slot + 1) * W], o_send.at[0, index, 0],
-                           o_recv.at[index, slot], at(s, q, c)).wait_recv()
-    for l in range(L):
-        for seq in range(Q):
-            here = jnp.logical_and(s == l, q == seq)
-
-            @pl.when(jnp.logical_not(here))
-            def _():
-                for index, (low, high) in enumerate(spans):
-                    remote(fresh_out.at[l, low:high, :], out.at[low:high, lane(own)], o_send.at[l, index, seq],
+                    remote(fresh_out.at[l, low:high, :], arrived.at[own, low:high, :], o_send.at[l, index, seq],
                            o_recv.at[index, own], at(l, seq, c)).wait_send()
     for copy in x_copies + g_copies:
         copy.wait_send()
@@ -596,24 +599,24 @@
     spans = 3
     result = pl.pallas_call(
         functools.partial(channel_kernel, sizes),
-        out_shape=jax.ShapeDtypeStruct((rows_out, channels), BF16),
-        in_specs=[pl.BlockSpec(memory_space=pl.ANY)] * 8,
+        out_shape=jax.ShapeDtypeStruct((rows_total * S * Q, W), F32),
+        in_specs=[pl.BlockSpec(memory_space=pltpu.HBM)] * 8,
         out_specs=pl.BlockSpec(memory_space=pltpu.VMEM),
         scratch_shapes=[
             V((M, R, channels), BF16), V((M, T, W), BF16), V((M, T, W), BF16),
-            V((L, 3, KS, W), F32), V((L, KL, W), F32), V((L, 1, W), F32), V((L, 1, W), F32),
+            V((L, 3 * KS, 1, W), F32), V((L, KL, W), F32), V((L, 1, W), F32), V((L, 1, W), F32),
             V(fw.shape, BF16), V(iv.shape, BF16),
             V((1, M * R), F32), V((Q * C, 1, M * R), F32), V((L, 1, M * T), F32), V((L, G, 1, M * T), F32),
             big(), big(), V((L, M, PAD + T, W), F32), big(), big(), big(),
             V((T, M * W), BF16), V((L, N, M * W), F32), big(), V((L, N, W), F32),
             V((T, M * W), BF16), V((N, M * W), F32), V((3, M, T + PAD, W), F32), V((M, T, W), F32),
-            V((M, T, W), F32), V((rows_out, W), F32), V((L, rows_out, W), BF16),
+            V((M, T, W), F32), V((rows_out, W), F32), V((L, rows_out, W), BF16), V((S * Q, rows_out, W), BF16),
             dma((9,)), dma((2, Q)), dma((2, Q)), dma((4,)), dma((4,)), dma((Q * C,)), dma((Q * C,)),
             dma((L, G)), dma((L, G)), dma((L, spans, Q)), dma((spans, S * Q)),
         ],
-        compiler_params=pltpu.CompilerParams(collective_id=0, has_side_effects=True, vmem_limit_bytes=40 * 1024 * 1024),
-    )(x, g, sf, lf, sk, ng, jnp.asarray(fw), jnp.asarray(iv))
-    return result[:rows_total].astype(F32)[None]
+        compiler_params=pltpu.CompilerParams(collective_id=0, has_side_effects=True, vmem_limit_bytes=60 * 1024 * 1024),
+    )(x, g, sf.reshape(3 * KS, 1, channels), lf, sk, ng, jnp.asarray(fw), jnp.asarray(iv))
+    return result.reshape(1, rows_total, channels)
 
 
 def solution(mesh):

time: 46.6 us -> 41.9 us (0.90)
  local copies, waits for them, and re-layouts: 7.33 us -> 2.32 us
  Pallas kernels: 38.9 us -> 39.4 us
    unnamed x15 -> x1, local copies, waits for them, and re-layouts: 5.87 us -> 2.32 us
    broadcast_in_dim x1 -> x0, local copies, waits for them, and re-layouts: 1.46 us -> none  [by_channels(): return result[:rows_total].astype(F32)[None]]
    pallas_call x1, Pallas kernels: 38.9 us -> 39.4 us  [by_channels(): pl.pallas_call(functools.partial(channel_kernel, sizes), out_shape=jax.Sh...]
where the time goes in v2:
time: 41.9 us; the launch traced here: 41.8 us
  Pallas kernels  39.4 us (94%)
  local copies, waits for them, and re-layouts  2.32 us (6%)
    pallas_call x1, Pallas kernels, by_channels(): pl.pallas_call(functools.partial(channel_kernel, sizes), out_shape=jax.Sh...  39.4 us
    unnamed x1, local copies, waits for them, and re-layouts  2.32 us

profile of v2, /device:TPU:0, one launch (start us, length us, event | category | flops | bytes accessed | tf_op | source)
XLA Modules:
  0.0 41.8 jit_solution(4682500483541278560)
XLA Ops:
  0.0 39.4 %shard_map.82 = f32[1208,128]{1,0:T(8,128)} custom-call(bf16[2,64,1024]{2,1,0:T(8,128)(2,1)} %x_in.1, bf16[2,64,1024]{2,1,0:T(8,128)(2,1)} %g_in.1, f32[21,1,1024]{2,1,0:T(1,128)} %bitcast.3, f32[1,128,1024]{2,1,0:T(8,128)} %lf_in.1, f32[1,1024]{1,0:T(1,128)} %sk_in.1, f32[1,1024]{1,0:T(1,128)} %ng_in.1, bf16[2,384,256]{2,1,0:T(8,128)(2,1)} %constant.4.clone.fw_in, ...), custom_call_target="tpu_custom_call" | custom-call | tf_op jit(solution)/shard_map/pallas_call | solution.py:600
  39.4 2.3 %copy.12 = f32[1,151,1024]{2,0,1:T(1,128)} copy(f32[1,151,1024]{2,0,1:T(1,128)} %bitcast.2) | data formatting | bytes 1236992

commit v3 on v2

--- a/solution.py
+++ b/solution.py
@@ -240,6 +240,7 @@
     H = N // 2
     L = S
     P_ALL = S * Q * C
+    STAGES = 2 * (L - 1)
     s, q, c = lax.axis_index("section"), lax.axis_index("seq"), lax.axis_index("chan")
     me = (s * Q + q) * C + c
     lane = lambda slot: pl.ds(pl.multiple_of(slot * W, W), W)
@@ -255,6 +256,10 @@
     def remote(src, dst, send, recv, where):
         return pltpu.make_async_remote_copy(src_ref=src, dst_ref=dst, send_sem=send, recv_sem=recv,
                                             device_id=where, device_id_type=pl.DeviceIdType.MESH)
+
+    barrier = pltpu.get_barrier_semaphore()
+    for offset in range(1, P_ALL):
+        pl.semaphore_signal(barrier, inc=1, device_id=peer(offset)[1], device_id_type=pl.DeviceIdType.MESH)
 
     own = q * S + s
     locals_ = [
@@ -268,14 +273,6 @@
     for copy in local_copies:
         copy.start()
 
-    barrier = pltpu.get_barrier_semaphore()
-
-    def greet(offset, carry):
-        pl.semaphore_signal(barrier, inc=1, device_id=peer(offset)[1], device_id_type=pl.DeviceIdType.MESH)
-        return carry
-
-    lax.fori_loop(1, P_ALL, greet, 0)
-
     local_copies[0].wait()
     for m in range(M):
         total = None
@@ -295,11 +292,8 @@
         p = lax.rem(q * C + c + offset, Q * C)
         return remote(part0_out, part0.at[q * C + c], p0_send.at[p], p0_recv.at[q * C + c], at(s, p // C, p % C))
 
-    def p0_start(offset, carry):
+    for offset in range(1, Q * C):
         p0_copy(offset).start()
-        return carry
-
-    lax.fori_loop(1, Q * C, p0_start, 0)
     x_copies, g_copies = [], []
     for offset in range(1, Q):
         to = lax.rem(q + offset, Q)
@@ -336,13 +330,10 @@
         f_hat[l] = mm3(fw[0, :, 0:KL], fw[1, :, 0:KL], lf[l])
         f_hat[l, 0:H, :] = f_hat[l, 0:H, :] + sk[l]
 
-    def p0_wait(offset, carry):
+    part0[q * C + c] = part0_out[...]
+    for offset in range(1, Q * C):
         p = lax.rem(q * C + c + offset, Q * C)
         remote(part0_out, part0.at[p], p0_send.at[p], p0_recv.at[p], at(s, p // C, p % C)).wait_recv()
-        return carry
-
-    part0[q * C + c] = part0_out[...]
-    lax.fori_loop(1, Q * C, p0_wait, 0)
     for seq in range(Q):
         row = part0[seq * C]
         for chan in range(1, C):
@@ -366,75 +357,65 @@
     def rounded(v):
         return v.astype(BF16).astype(F32)
 
-    def forward(l):
+    def lanes(m):
+        return slice(m * W, (m + 1) * W)
+
+    def inverse(product):
+        high, low = split(product)
+        both = mm(iv[0], jnp.concatenate([high, low], axis=1))
+        return both[:, 0:W] + (both[:, W:2 * W] + mm(iv[1], high))
+
+    def forward(l, m):
         gain = ng[l]
-        for m in range(M):
-            def norm_chunk(t):
-                v = xf[l, m, pl.ds(t, CHUNK), :] * scale[l, m, pl.ds(t, CHUNK), :] * gain
-                normed[l, m, pl.ds(t + PAD, CHUNK), :] = rounded(v)
-
-            chunks(norm_chunk)
+
+        def norm_chunk(t):
+            v = xf[l, m, pl.ds(t, CHUNK), :] * scale[l, m, pl.ds(t, CHUNK), :] * gain
+            normed[l, m, pl.ds(t + PAD, CHUNK), :] = rounded(v)
+
+        chunks(norm_chunk)
         taps = [[sf[l, i * KS + j] for j in range(KS)] for i in range(3)]
-        for m in range(M):
-            def short_chunk(t):
-                sums = [None] * 3
-                for j in range(KS):
-                    shifted_rows = normed[l, m, pl.ds(t + PAD - j, CHUNK), :]
-                    for i in range(3):
-                        term = taps[i][j] * shifted_rows
-                        sums[i] = term if sums[i] is None else sums[i] + term
-                query[l, m, pl.ds(t, CHUNK), :] = sums[0]
-                key[l, m, pl.ds(t, CHUNK), :] = sums[1]
-                value[l, m, pl.ds(t, CHUNK), :] = sums[2]
-                mixed[pl.ds(t, CHUNK), m * W:(m + 1) * W] = (sums[1] * sums[2]).astype(BF16)
-
-            chunks(short_chunk)
-        m_hat[l] = mm(fw[0], mixed[...]) + mm(fw[1], mixed[...])
-        pieces = []
-        for m in range(M):
-            fr, fi = f_hat[l, 0:H, :], f_hat[l, H:N, :]
-            mr, mi = m_hat[l, 0:H, m * W:(m + 1) * W], m_hat[l, H:N, m * W:(m + 1) * W]
-            pieces.append(jnp.concatenate([fr * mr - fi * mi, fr * mi + fi * mr], axis=0))
-        result = mm3(iv[0], iv[1], jnp.concatenate(pieces, axis=1))
-        for m in range(M):
-            filtered[l, m] = result[:, m * W:(m + 1) * W]
-
-    def exchange(stage, rows_of):
-        part_out[stage] = jnp.concatenate([lane_sums(rows_of(m)) for m in range(M)], axis=1)
-
-        def send(offset, carry):
+
+        def short_chunk(t):
+            sums = [None] * 3
+            for j in range(KS):
+                shifted_rows = normed[l, m, pl.ds(t + PAD - j, CHUNK), :]
+                for i in range(3):
+                    term = taps[i][j] * shifted_rows
+                    sums[i] = term if sums[i] is None else sums[i] + term
+            query[l, m, pl.ds(t, CHUNK), :] = sums[0]
+            key[l, m, pl.ds(t, CHUNK), :] = sums[1]
+            value[l, m, pl.ds(t, CHUNK), :] = sums[2]
+            mixed[pl.ds(t, CHUNK), lanes(m)] = (sums[1] * sums[2]).astype(BF16)
+
+        chunks(short_chunk)
+        m_hat[l, :, lanes(m)] = mm(fw[0], mixed[:, lanes(m)]) + mm(fw[1], mixed[:, lanes(m)])
+        fr, fi = f_hat[l, 0:H, :], f_hat[l, H:N, :]
+        mr, mi = m_hat[l, 0:H, lanes(m)], m_hat[l, H:N, lanes(m)]
+        filtered[l, m] = inverse(jnp.concatenate([fr * mr - fi * mi, fr * mi + fi * mr], axis=0))
+
+    def exchange(stage, m, rows):
+        i = stage * M + m
+        part_out[i] = lane_sums(rows)
+        for offset in range(1, P_ALL):
             p, where = peer(offset)
-            remote(part_out.at[stage], part.at[stage, me], p_send.at[stage, p], p_recv.at[stage, me], where).start()
-            return carry
-
-        lax.fori_loop(1, P_ALL, send, 0)
-
-    def exchanged(stage):
-        part[stage, me] = part_out[stage]
-
-        def wait(offset, carry):
+            remote(part_out.at[i], part.at[i, me], p_send.at[i, p], p_recv.at[i, me], where).start()
+
+    def exchanged(stage, m):
+        i = stage * M + m
+        part[i, me] = part_out[i]
+        for offset in range(1, P_ALL):
             p, where = peer(offset)
-            remote(part_out.at[stage], part.at[stage, p], p_send.at[stage, p], p_recv.at[stage, p], where).wait_recv()
-            return carry
-
-        lax.fori_loop(1, P_ALL, wait, 0)
-        rows = [part[stage, p] for p in range(P_ALL)]
+            remote(part_out.at[i], part.at[i, p], p_send.at[i, p], p_recv.at[i, p], where).wait_recv()
+        rows = [part[i, p] for p in range(P_ALL)]
         while len(rows) > 1:
             rows = [a + b for a, b in zip(rows[::2], rows[1::2])] + ([rows[-1]] if len(rows) % 2 else [])
         return rows[0]
 
-    for l in range(L):
-        forward(l)
+    def forward_and_on(l, m):
+        forward(l, m)
         if l < L - 1:
-            for m in range(M):
-                xf[l + 1, m] = rounded(xf[l, m] + query[l, m] * filtered[l, m])
-            exchange(l, lambda m: xf[l + 1, m] * xf[l + 1, m])
-            root = lax.rsqrt(exchanged(l) / D + EPSILON)
-            for m in range(M):
-                scale[l + 1, m] = as_columns(root[:, m * T:(m + 1) * T], W)
-
-    for copy in g_copies:
-        copy.wait_recv()
+            xf[l + 1, m] = rounded(xf[l, m] + query[l, m] * filtered[l, m])
+            exchange(l, m, xf[l + 1, m] * xf[l + 1, m])
 
     slots = S * Q
     rows_total = 3 * KS + KL + 2
@@ -460,56 +441,48 @@
     early_high = (3 * KS + KL) // 16 * 16
     late_high = fresh_out.shape[1]
     spans = [(early_low, early_high), (0, early_low), (early_high, late_high)]
-    stages = L - 1
-    for l in reversed(range(L)):
-        top = l == L - 1
+
+    def cotangent(l, m):
+        return g_all[m].astype(F32) if l == L - 1 else e_one[l, m]
+
+    def backward_filtered(l, m):
+        e = cotangent(l, m)
+        d_str[0, m, 0:T, :] = rounded(e * filtered[l, m])
+        d_fil[:, lanes(m)] = (e * query[l, m]).astype(BF16)
+        d_hat[:, lanes(m)] = mm(fw[0], d_fil[:, lanes(m)]) + mm(fw[1], d_fil[:, lanes(m)])
+
+    def backward_normed(l, m):
+        fr, fi = f_hat[l, 0:H, :], f_hat[l, H:N, :]
+        dr, di = d_hat[0:H, lanes(m)], d_hat[H:N, lanes(m)]
+        d_mix = inverse(jnp.concatenate([fr * dr + fi * di, fr * di - fi * dr], axis=0))
+        d_str[1, m, 0:T, :] = rounded(d_mix * value[l, m])
+        d_str[2, m, 0:T, :] = rounded(d_mix * key[l, m])
+        taps = [[sf[l, i * KS + j] for j in range(KS)] for i in range(3)]
+
+        def normed_chunk(t):
+            total = None
+            for i in range(3):
+                for j in range(KS):
+                    term = taps[i][j] * d_str[i, m, pl.ds(t + j, CHUNK), :]
+                    total = term if total is None else total + term
+            d_nor[m, pl.ds(t, CHUNK), :] = total
+
+        chunks(normed_chunk)
+
+    def long_gradient(l):
+        re, im = None, None
         for m in range(M):
-            e = g_all[m].astype(F32) if top else e_one[m]
-            d_str[0, m, 0:T, :] = rounded(e * filtered[l, m])
-            d_fil[:, m * W:(m + 1) * W] = (e * query[l, m]).astype(BF16)
-        d_hat[...] = mm(fw[0], d_fil[...]) + mm(fw[1], d_fil[...])
-
-        def long_gradient():
-            re, im = None, None
-            for m in range(M):
-                dr, di = d_hat[0:H, m * W:(m + 1) * W], d_hat[H:N, m * W:(m + 1) * W]
-                mr, mi = m_hat[l, 0:H, m * W:(m + 1) * W], m_hat[l, H:N, m * W:(m + 1) * W]
-                a, b = dr * mr + di * mi, di * mr - dr * mi
-                re, im = (a, b) if re is None else (re + a, im + b)
-            taps_grad = mm3(iv[0, 0:KL, :], iv[1, 0:KL, :], jnp.concatenate([re, im], axis=0))
-            fresh[3 * KS:3 * KS + KL, :] = taps_grad
-            fresh[3 * KS + KL:3 * KS + KL + 1, :] = taps_grad[0:1]
-            fresh_out[l, early_low:early_high, :] = fresh[early_low:early_high, :].astype(BF16)
-            send_rows(l, 0, early_low, early_high)
-
-        if not top:
-            long_gradient()
-        pieces = []
-        for m in range(M):
-            fr, fi = f_hat[l, 0:H, :], f_hat[l, H:N, :]
-            dr, di = d_hat[0:H, m * W:(m + 1) * W], d_hat[H:N, m * W:(m + 1) * W]
-            pieces.append(jnp.concatenate([fr * dr + fi * di, fr * di - fi * dr], axis=0))
-        d_mix = mm3(iv[0], iv[1], jnp.concatenate(pieces, axis=1))
-        for m in range(M):
-            d_mix_m = d_mix[:, m * W:(m + 1) * W]
-            d_str[1, m, 0:T, :] = rounded(d_mix_m * value[l, m])
-            d_str[2, m, 0:T, :] = rounded(d_mix_m * key[l, m])
-        taps = [[sf[l, i * KS + j] for j in range(KS)] for i in range(3)]
-        for m in range(M):
-            def normed_chunk(t):
-                total = None
-                for i in range(3):
-                    for j in range(KS):
-                        term = taps[i][j] * d_str[i, m, pl.ds(t + j, CHUNK), :]
-                        total = term if total is None else total + term
-                d_nor[m, pl.ds(t, CHUNK), :] = total
-
-            chunks(normed_chunk)
-        gain = ng[l]
-        if l > 0:
-            exchange(stages, lambda m: gain * d_nor[m] * xf[l, m])
-        if top:
-            long_gradient()
+            dr, di = d_hat[0:H, lanes(m)], d_hat[H:N, lanes(m)]
+            mr, mi = m_hat[l, 0:H, lanes(m)], m_hat[l, H:N, lanes(m)]
+            a, b = dr * mr + di * mi, di * mr - dr * mi
+            re, im = (a, b) if re is None else (re + a, im + b)
+        taps_grad = mm3(iv[0, 0:KL, :], iv[1, 0:KL, :], jnp.concatenate([re, im], axis=0))
+        fresh[3 * KS:3 * KS + KL, :] = taps_grad
+        fresh[3 * KS + KL:3 * KS + KL + 1, :] = taps_grad[0:1]
+        fresh_out[l, early_low:early_high, :] = fresh[early_low:early_high, :].astype(BF16)
+        send_rows(l, 0, early_low, early_high)
+
+    def short_gradients(l):
         fold = lambda v: jnp.sum(v.reshape(CHUNK // 8, 8, W), axis=0)
         zeros = tuple(jnp.zeros((8, W), F32) for _ in range(3 * KS + 1))
 
@@ -534,12 +507,37 @@
             low, high = spans[index]
             fresh_out[l, low:high, :] = fresh[low:high, :].astype(BF16)
             send_rows(l, index, low, high)
+
+    for l in range(L - 1):
+        for m in range(M):
+            if l > 0:
+                scale[l, m] = as_columns(lax.rsqrt(exchanged(l - 1, m) / D + EPSILON), W)
+            forward_and_on(l, m)
+    top = L - 1
+    for copy in g_copies:
+        copy.wait_recv()
+    for m in range(M):
+        scale[top, m] = as_columns(lax.rsqrt(exchanged(top - 1, m) / D + EPSILON), W)
+        forward(top, m)
+        backward_filtered(top, m)
+        backward_normed(top, m)
+        exchange(top, m, ng[top] * d_nor[m] * xf[top, m])
+    long_gradient(top)
+    for l in reversed(range(L)):
+        short_gradients(l)
         if l > 0:
-            norm_row = exchanged(stages) / D
+            stage = 2 * top - l
+            below = l - 1
             for m in range(M):
-                term = as_columns(norm_row[:, m * T:(m + 1) * T], W)
+                term = as_columns(exchanged(stage, m) / D, W)
                 r = scale[l, m]
-                e_one[m] = rounded(g_all[m].astype(F32) + r * gain * d_nor[m] - xf[l, m] * (r * r * r) * term)
+                e_one[below, m] = rounded(cotangent(l, m) + r * ng[l] * d_nor[m] - xf[l, m] * (r * r * r) * term)
+                backward_filtered(below, m)
+                if m == M - 1:
+                    long_gradient(below)
+                backward_normed(below, m)
+                if below > 0:
+                    exchange(stage + 1, m, ng[below] * d_nor[m] * xf[below, m])
 
     for index, (low, high) in enumerate(spans):
         for slot in range(slots):
@@ -565,7 +563,7 @@
         return carry
 
     lax.fori_loop(1, Q * C, p0_sent, 0)
-    for stage in range(L):
+    for stage in range(STAGES * M):
         def sent(offset, carry):
             p, where = peer(offset)
             remote(part_out.at[stage], part.at[stage, me], p_send.at[stage, p], p_recv.at[stage, me], where).wait_send()
@@ -597,6 +595,8 @@
     sizes = (S, Q, C, M, R, W, KS, KL, D)
     big = lambda: V((L, M, T, W), F32)
     spans = 3
+    stages = 2 * (L - 1)
+    pinned = [pltpu.with_memory_space_constraint(a, pltpu.HBM) for a in (x, g, sf.reshape(3 * KS, 1, channels), lf, sk, ng, jnp.asarray(fw), jnp.asarray(iv))]
     result = pl.pallas_call(
         functools.partial(channel_kernel, sizes),
         out_shape=jax.ShapeDtypeStruct((rows_total * S * Q, W), F32),
@@ -606,16 +606,16 @@
             V((M, R, channels), BF16), V((M, T, W), BF16), V((M, T, W), BF16),
             V((L, 3 * KS, 1, W), F32), V((L, KL, W), F32), V((L, 1, W), F32), V((L, 1, W), F32),
             V(fw.shape, BF16), V(iv.shape, BF16),
-            V((1, M * R), F32), V((Q * C, 1, M * R), F32), V((L, 1, M * T), F32), V((L, G, 1, M * T), F32),
+            V((1, M * R), F32), V((Q * C, 1, M * R), F32), V((stages * M, 1, T), F32), V((stages * M, G, 1, T), F32),
             big(), big(), V((L, M, PAD + T, W), F32), big(), big(), big(),
             V((T, M * W), BF16), V((L, N, M * W), F32), big(), V((L, N, W), F32),
             V((T, M * W), BF16), V((N, M * W), F32), V((3, M, T + PAD, W), F32), V((M, T, W), F32),
-            V((M, T, W), F32), V((rows_out, W), F32), V((L, rows_out, W), BF16), V((S * Q, rows_out, W), BF16),
+            V((L, M, T, W), F32), V((rows_out, W), F32), V((L, rows_out, W), BF16), V((S * Q, rows_out, W), BF16),
             dma((9,)), dma((2, Q)), dma((2, Q)), dma((4,)), dma((4,)), dma((Q * C,)), dma((Q * C,)),
-            dma((L, G)), dma((L, G)), dma((L, spans, Q)), dma((spans, S * Q)),
+            dma((stages * M, G)), dma((stages * M, G)), dma((L, spans, Q)), dma((spans, S * Q)),
         ],
-        compiler_params=pltpu.CompilerParams(collective_id=0, has_side_effects=True, vmem_limit_bytes=60 * 1024 * 1024),
-    )(x, g, sf.reshape(3 * KS, 1, channels), lf, sk, ng, jnp.asarray(fw), jnp.asarray(iv))
+        compiler_params=pltpu.CompilerParams(collective_id=0, has_side_effects=True, vmem_limit_bytes=40 * 1024 * 1024),
+    )(*pinned)
     return result.reshape(1, rows_total, channels)
 
 

time: 41.9 us -> 40.7 us (0.971)
  local copies, waits for them, and re-layouts: 2.32 us -> 0.83 us
    unnamed x1, local copies, waits for them, and re-layouts: 2.32 us -> 0.83 us
where the time goes in v3:
time: 40.7 us; the launch traced here: 40.6 us
  Pallas kernels  39.7 us (98%)
  local copies, waits for them, and re-layouts  0.83 us (2%)
    pallas_call x1, Pallas kernels, by_channels(): pl.pallas_call(functools.partial(channel_kernel, sizes), out_shape=jax.Sh...  39.7 us
    unnamed x1, local copies, waits for them, and re-layouts  0.83 us

profile of v3, /device:TPU:0, one launch (start us, length us, event | category | flops | bytes accessed | tf_op | source)
XLA Modules:
  0.0 40.6 jit_solution(16725361648596937885)
XLA Ops:
  0.0 39.7 %shard_map.82 = f32[1208,128]{1,0:T(8,128)S(1)} custom-call(bf16[2,64,1024]{2,1,0:T(8,128)(2,1)} %x_in.1, bf16[2,64,1024]{2,1,0:T(8,128)(2,1)} %g_in.1, f32[21,1,1024]{2,1,0:T(1,128)} %bitcast.3, f32[1,128,1024]{2,1,0:T(8,128)} %lf_in.1, f32[1,1024]{1,0:T(1,128)} %sk_in.1, f32[1,1024]{1,0:T(1,128)} %ng_in.1, bf16[2,384,256]{2,1,0:T(8,128)(2,1)} %constant.4.clone.fw_in, ...), custom_call_target="tpu_custom_call" | custom-call | tf_op jit(solution)/shard_map/pallas_call | solution.py:600
  39.7 0.8 %copy.12 = f32[1,151,1024]{2,0,1:T(1,128)} copy(f32[1,151,1024]{2,0,1:T(1,128)S(1)} %bitcast.2) | data formatting | bytes 1236992

commit v4 on v3

--- a/solution.py
+++ b/solution.py
@@ -298,10 +298,13 @@
     for offset in range(1, Q):
         to = lax.rem(q + offset, Q)
         src_slot = to * S + s
-        x_copies.append(remote(x_in.at[:, :, lane(src_slot)], x_all.at[:, rows_at(q), :], x_send.at[0, offset], x_recv.at[0, offset], at(s, to, c)))
-        g_copies.append(remote(g_in.at[:, :, lane(src_slot)], g_all.at[:, rows_at(q), :], x_send.at[1, offset], x_recv.at[1, offset], at(s, to, c)))
-    for copy in x_copies:
-        copy.start()
+        for m in range(M):
+            x_copies.append((m, remote(x_in.at[m, :, lane(src_slot)], x_all.at[m, rows_at(q), :], x_send.at[m, offset], x_recv.at[m, offset], at(s, to, c))))
+        g_copies.append(remote(g_in.at[:, :, lane(src_slot)], g_all.at[:, rows_at(q), :], x_send.at[M, offset], x_recv.at[M, offset], at(s, to, c)))
+    x_copies = [[copy for index, copy in x_copies if index == m] for m in range(M)]
+    for m in range(M):
+        for copy in x_copies[m]:
+            copy.start()
     mate = 1 - s
     theirs = q * S + mate
     f_copies = [
@@ -312,8 +315,6 @@
         ])
     ]
     for copy in f_copies:
-        copy.start()
-    for copy in g_copies:
         copy.start()
 
     for l in range(L):
@@ -341,18 +342,13 @@
         columns = as_columns(lax.rsqrt(row / D + EPSILON), W)
         for m in range(M):
             scale[0, m, seq * R:(seq + 1) * R, :] = columns[m * R:(m + 1) * R]
-    for copy in x_copies:
-        copy.wait_recv()
-    for m in range(M):
-        for t in range(0, T, R):
-            xf[0, m, t:t + R, :] = x_all[m, t:t + R, :].astype(F32)
 
     def chunks(body):
         def step(i, carry):
             body(pl.multiple_of(i * CHUNK, CHUNK))
             return carry
 
-        lax.fori_loop(0, T // CHUNK, step, 0)
+        lax.fori_loop(0, T // CHUNK, step, 0, unroll=True)
 
     def rounded(v):
         return v.astype(BF16).astype(F32)
@@ -510,15 +506,22 @@
 
     for l in range(L - 1):
         for m in range(M):
+            if l == 0:
+                for copy in x_copies[m]:
+                    copy.wait_recv()
+                xf[0, m] = x_all[m].astype(F32)
             if l > 0:
                 scale[l, m] = as_columns(lax.rsqrt(exchanged(l - 1, m) / D + EPSILON), W)
             forward_and_on(l, m)
     top = L - 1
     for copy in g_copies:
-        copy.wait_recv()
+        copy.start()
     for m in range(M):
         scale[top, m] = as_columns(lax.rsqrt(exchanged(top - 1, m) / D + EPSILON), W)
         forward(top, m)
+        if m == 0:
+            for copy in g_copies:
+                copy.wait_recv()
         backward_filtered(top, m)
         backward_normed(top, m)
         exchange(top, m, ng[top] * d_nor[m] * xf[top, m])
@@ -555,7 +558,7 @@
                 for index, (low, high) in enumerate(spans):
                     remote(fresh_out.at[l, low:high, :], arrived.at[own, low:high, :], o_send.at[l, index, seq],
                            o_recv.at[index, own], at(l, seq, c)).wait_send()
-    for copy in x_copies + g_copies:
+    for copy in sum(x_copies, []) + g_copies:
         copy.wait_send()
 
     def p0_sent(offset, carry):
@@ -611,7 +614,7 @@
             V((T, M * W), BF16), V((L, N, M * W), F32), big(), V((L, N, W), F32),
             V((T, M * W), BF16), V((N, M * W), F32), V((3, M, T + PAD, W), F32), V((M, T, W), F32),
             V((L, M, T, W), F32), V((rows_out, W), F32), V((L, rows_out, W), BF16), V((S * Q, rows_out, W), BF16),
-            dma((9,)), dma((2, Q)), dma((2, Q)), dma((4,)), dma((4,)), dma((Q * C,)), dma((Q * C,)),
+            dma((9,)), dma((M + 1, Q)), dma((M + 1, Q)), dma((4,)), dma((4,)), dma((Q * C,)), dma((Q * C,)),
             dma((stages * M, G)), dma((stages * M, G)), dma((L, spans, Q)), dma((spans, S * Q)),
         ],
         compiler_params=pltpu.CompilerParams(collective_id=0, has_side_effects=True, vmem_limit_bytes=40 * 1024 * 1024),

time: 40.7 us -> 38.7 us (0.951)
  Pallas kernels: 39.7 us -> 37.7 us
    pallas_call x1, Pallas kernels: 39.7 us -> 37.7 us  [by_channels(): pl.pallas_call(functools.partial(channel_kernel, sizes), out_shape=jax.Sh...]
where the time goes in v4:
time: 38.7 us; the launch traced here: 38.6 us
  Pallas kernels  37.7 us (97%)
  local copies, waits for them, and re-layouts  0.83 us (2%)
    pallas_call x1, Pallas kernels, by_channels(): pl.pallas_call(functools.partial(channel_kernel, sizes), out_shape=jax.Sh...  37.7 us
    unnamed x1, local copies, waits for them, and re-layouts  0.83 us

profile of v4, /device:TPU:0, one launch (start us, length us, event | category | flops | bytes accessed | tf_op | source)
XLA Modules:
  0.0 38.6 jit_solution(15176087333943389385)
XLA Ops:
  0.0 37.7 %shard_map.82 = f32[1208,128]{1,0:T(8,128)S(1)} custom-call(bf16[2,64,1024]{2,1,0:T(8,128)(2,1)} %x_in.1, bf16[2,64,1024]{2,1,0:T(8,128)(2,1)} %g_in.1, f32[21,1,1024]{2,1,0:T(1,128)} %bitcast.3, f32[1,128,1024]{2,1,0:T(8,128)} %lf_in.1, f32[1,1024]{1,0:T(1,128)} %sk_in.1, f32[1,1024]{1,0:T(1,128)} %ng_in.1, bf16[2,384,256]{2,1,0:T(8,128)(2,1)} %constant.4.clone.fw_in, ...), custom_call_target="tpu_custom_call" | custom-call | tf_op jit(solution)/shard_map/pallas_call | solution.py:603
  37.7 0.8 %copy.12 = f32[1,151,1024]{2,0,1:T(1,128)} copy(f32[1,151,1024]{2,0,1:T(1,128)S(1)} %bitcast.2) | data formatting | bytes 1236992
